TPU v7x, 32 devices: a whole 2x2x4 slice. The times are simulated.
32 devices in a mesh: rows: 16 (over z, y, x), cols: 2 (over core).
Axes of the slice: x: 2, y: 2, z: 4, core: 2. Of those that a mesh axis runs over, the one named last changes fastest.
Arguments:
- points: bfloat16 [20480, 512], P('rows', 'cols'), may hold values from -6 to 6
- factor: bfloat16 [20480, 1024], P('rows', 'cols'), may hold values from -2 to 2
- weights: float32 [20480], P('rows'), may hold values from -4 to 4
- pivot_slots: int32 [4, 128], replicated, may hold values from 0 to 1279, as said below
- pivot_owners: int32 [4, 128], replicated, may hold values from 0 to 15
Outputs:
- new_panels: bfloat16 [20480, 512], P('rows', 'cols')
- gram_old: float32 [512, 1024], P('rows', 'cols')
- gram_new: float32 [512, 512], P('rows', 'cols')
Inputs may be any that keep to these rules, and one draw needn't show every extreme that they name: Pivot k of panel q is row pivot_slots[q,k] of the block of device pivot_owners[q,k]; the pivots of all panels together are distinct points.
All inputs are finite; a program needn't handle non-finite values.
Results may differ from a plain program's by a relative error of at most 0.009.
Values may be sent and summed in bfloat16 or wider, within the bound.
A program may use at most 64 MiB of HBM per device.

v0:
```python
import math

import jax
import jax.numpy as jnp
from jax import lax
from jax.sharding import PartitionSpec as P

F = 512
R = 1024


RIDGE_LEVEL = 1.0


def body(points, factor, weights, pivot_slots, pivot_owners):
    rows_here = points.shape[0]
    panel = pivot_slots.shape[1]
    panel_count = pivot_slots.shape[0]
    device = lax.axis_index("rows")
    column = lax.axis_index("cols")
    halves = lax.axis_size("cols")
    total_rows = rows_here * lax.axis_size("rows")
    identity = jnp.eye(panel, dtype=jnp.float32)
    half_rows = rows_here // halves
    full_points, full_factor = (
        lax.all_to_all(points, "cols", split_axis=0, concat_axis=1, tiled=True),
        lax.all_to_all(factor, "cols", split_axis=0, concat_axis=1, tiled=True),
    )
    local_ids = device * rows_here + column * half_rows + jnp.arange(half_rows, dtype=jnp.int32)
    local_norms = jnp.sum(jnp.square(full_points.astype(jnp.float32)), axis=1)
    built_half = jnp.zeros((half_rows, panel_count * panel), jnp.bfloat16)
    for index in range(panel_count):
        slots = pivot_slots[index]
        owners = pivot_owners[index]
        pivot_ids = owners * rows_here + slots
        chosen = ((owners == device) & (slots // half_rows == column))[:, None]
        local_slots = slots % half_rows
        sel_points = jnp.where(
            chosen, jnp.take(full_points, local_slots, axis=0).astype(jnp.float32), 0.0
        )
        sel_factor = jnp.where(
            chosen, jnp.take(full_factor, local_slots, axis=0).astype(jnp.float32), 0.0
        )
        sel_built = jnp.where(
            chosen, jnp.take(built_half, local_slots, axis=0).astype(jnp.float32), 0.0
        )
        sel_points, sel_factor, sel_built = lax.psum(
            (sel_points, sel_factor, sel_built), ("rows", "cols")
        )
        piv_norms = jnp.sum(jnp.square(sel_points), axis=1)
        piv_points = sel_points.astype(jnp.bfloat16)
        piv_factor = sel_factor.astype(jnp.bfloat16)
        piv_built = sel_built.astype(jnp.bfloat16)
        cross = jnp.dot(full_points, piv_points.T, preferred_element_type=jnp.float32)
        dist = local_norms[:, None] + piv_norms[None, :] - 2.0 * cross
        schur = jnp.dot(full_factor, piv_factor.T, preferred_element_type=jnp.float32)
        block_dist = (
            piv_norms[:, None]
            + piv_norms[None, :]
            - 2.0 * jnp.dot(piv_points, piv_points.T, preferred_element_type=jnp.float32)
        )
        block_schur = jnp.dot(piv_factor, piv_factor.T, preferred_element_type=jnp.float32)
        ridge = jnp.where(local_ids[:, None] == pivot_ids[None, :], RIDGE_LEVEL, 0.0)
        columns = (
            jnp.exp(-dist / F)
            + ridge
            + schur / (3.0 * R)
            - jnp.dot(built_half, piv_built.T, preferred_element_type=jnp.float32)
        )
        block = (
            jnp.exp(-block_dist / F)
            + RIDGE_LEVEL * identity
            + block_schur / (3.0 * R)
            - jnp.dot(piv_built, piv_built.T, preferred_element_type=jnp.float32)
        )
        lower = jnp.linalg.cholesky(block)
        inverse = lax.linalg.triangular_solve(lower, identity, left_side=True, lower=True)
        fresh = jnp.dot(columns, inverse.T, precision=lax.Precision.HIGHEST).astype(jnp.bfloat16)
        built_half = built_half.at[:, index * panel : (index + 1) * panel].set(fresh)
    built = lax.all_gather(built_half, "cols", axis=0, tiled=True)
    width = built.shape[1] // halves
    own_columns = lax.dynamic_slice_in_dim(built, column * width, width, 1)
    weighted = (built.astype(jnp.float32) * weights[:, None]).astype(jnp.bfloat16)
    dims = (((0,), (0,)), ((), ()))
    old_part = lax.dot_general(weighted, factor, dims, preferred_element_type=jnp.float32)
    new_part = lax.dot_general(weighted, own_columns, dims, preferred_element_type=jnp.float32)
    old_full, new_full = lax.psum((old_part, new_part), "rows")
    out_rows = old_part.shape[0] // lax.axis_size("rows")
    old_sum = lax.dynamic_slice_in_dim(old_full, device * out_rows, out_rows, 0)
    new_sum = lax.dynamic_slice_in_dim(new_full, device * out_rows, out_rows, 0)
    scale = panel / math.sqrt(total_rows)
    return (own_columns, old_sum * scale, new_sum * scale)


def solution(mesh):
    return jax.shard_map(
        body,
        mesh=mesh,
        in_specs=(P("rows", "cols"), P("rows", "cols"), P("rows"), P(), P()),
        out_specs=(P("rows", "cols"), P("rows", "cols"), P("rows", "cols")),
        check_vma=False,
    )
```

profile of v0, /device:TPU:0, one launch (start us, length us, event | category | flops | bytes accessed | tf_op | source)
XLA Modules:
  0.0 558.4 jit_solution(13490840416334126539)
XLA Ops:
  7.2 3.5 all-to-all-start
  12.5 3.6 all-to-all-start.1
  20.2 1.6 gather_fusion.2
  30.1 1.7 gather_fusion.1
  33.4 1.7 gather_fusion.7
  37.3 1.9 convert_select_fusion.2
  39.3 1.9 convert_select_fusion.1
  42.1 50.4 %all-reduce.17 = (bf16[128,1024]{1,0:T(8,128)(2,1)S(1)}, bf16[128,512]{1,0:T(8,128)(2,1)S(1)}) all-reduce(f32[128,1024]{1,0:T(8,128)S(1)} %convert_select_fusion.3, f32[128,512]{1,0:T(8,128)} %get-tuple-element.94), channel_id=1, replica_groups=mesh['rows'=16,'cols'=2] {'rows','cols'}, use_global_device_ids=true, to_apply=%region_4.7 | all-reduce | flops 196608 | bytes 1179648 | tf_op jit(solution)/shard_map/psum | solution.py:47
  95.6 65.8 %all-reduce.14.cloned.1.call-done = (f32[128,512]{1,0:T(8,128)}, f32[128,512]{1,0:T(8,128)}, f32[128,512]{1,0:T(8,128)}, f32[128,512]{1,0:T(8,128)}) async-done(((f32[128,512]{1,0:T(8,128)}, f32[128,512]{1,0:T(8,128)}, f32[128,512]{1,0:T(8,128)}, f32[128,512]{1,0:T(8,128)}), (f32[128,512]{1,0:T(8,128)}, f32[128,512]{1,0:T(8,128)}, f32[128,512]{1,0:T(8,128)}, ...) | async-done | bytes 1048592 | tf_op jit(solution)/shard_map/psum | solution.py:47
  164.1 11.7 %cholesky.74 = f32[128,128]{1,0:T(8,128)S(1)} custom-call(f32[128,128]{1,0:T(8,128)S(1)} %fusion.93), custom_call_target="Cholesky" | custom-call | tf_op jit(solution)/shard_map/jit(cholesky)/cholesky | solution.py:76
  177.1 9.8 %custom-call.8 = f32[1,128,128]{1,2,0:T(8,128)S(1)} custom-call(f32[1,128,128]{2,1,0:T(8,128)S(1)} %fusion.82), custom_call_target="InvertDiagBlocksLowerTriangular" | custom-call | tf_op jit(solution)/shard_map/triangular_solve/custom-call.0 | solution.py:77
  190.2 47.3 %all-reduce.18 = (bf16[128,1024]{1,0:T(8,128)(2,1)S(1)}, bf16[128,512]{1,0:T(8,128)(2,1)S(1)}) all-reduce(f32[128,1024]{1,0:T(8,128)} %convert_select_fusion.2, f32[128,512]{1,0:T(8,128)S(1)} %convert_select_fusion.8), channel_id=1, replica_groups=mesh['rows'=16,'cols'=2] {'rows','cols'}, use_global_device_ids=true, to_apply=%region_11.16 | all-reduce | flops 196608 | bytes 1179648 | tf_op jit(solution)/shard_map/psum | solution.py:47
  239.6 11.7 %cholesky.85 = f32[128,128]{1,0:T(8,128)S(1)} custom-call(f32[128,128]{1,0:T(8,128)S(1)} %fusion.91), custom_call_target="Cholesky" | custom-call | tf_op jit(solution)/shard_map/jit(cholesky)/cholesky | solution.py:76
  252.7 9.8 %custom-call.9 = f32[1,128,128]{1,2,0:T(8,128)S(1)} custom-call(f32[1,128,128]{2,1,0:T(8,128)S(1)} %fusion.83), custom_call_target="InvertDiagBlocksLowerTriangular" | custom-call | tf_op jit(solution)/shard_map/triangular_solve/custom-call.0 | solution.py:77
  266.7 45.8 %all-reduce.19 = (bf16[128,1024]{1,0:T(8,128)(2,1)S(1)}, bf16[128,512]{1,0:T(8,128)(2,1)}) all-reduce(f32[128,1024]{1,0:T(8,128)} %convert_select_fusion.1, f32[128,512]{1,0:T(8,128)S(1)} %convert_select_fusion.6), channel_id=1, replica_groups=mesh['rows'=16,'cols'=2] {'rows','cols'}, use_global_device_ids=true, to_apply=%region_16.21 | all-reduce | flops 196608 | bytes 1179648 | tf_op jit(solution)/shard_map/psum | solution.py:47
  314.1 11.7 %cholesky.96 = f32[128,128]{1,0:T(8,128)S(1)} custom-call(f32[128,128]{1,0:T(8,128)S(1)} %fusion.89), custom_call_target="Cholesky" | custom-call | tf_op jit(solution)/shard_map/jit(cholesky)/cholesky | solution.py:76
  327.2 9.8 %custom-call.10 = f32[1,128,128]{1,2,0:T(8,128)S(1)} custom-call(f32[1,128,128]{2,1,0:T(8,128)S(1)} %fusion.84), custom_call_target="InvertDiagBlocksLowerTriangular" | custom-call | tf_op jit(solution)/shard_map/triangular_solve/custom-call.0 | solution.py:77
  340.9 47.2 %all-reduce.20 = (bf16[128,1024]{1,0:T(8,128)(2,1)S(1)}, bf16[128,512]{1,0:T(8,128)(2,1)}) all-reduce(f32[128,1024]{1,0:T(8,128)} %convert_select_fusion, f32[128,512]{1,0:T(8,128)S(1)} %convert_select_fusion.4), channel_id=1, replica_groups=mesh['rows'=16,'cols'=2] {'rows','cols'}, use_global_device_ids=true, to_apply=%region_20.25 | all-reduce | flops 196608 | bytes 1179648 | tf_op jit(solution)/shard_map/psum | solution.py:47
  389.7 11.7 %cholesky.107 = f32[128,128]{1,0:T(8,128)S(1)} custom-call(f32[128,128]{1,0:T(8,128)S(1)} %fusion.87), custom_call_target="Cholesky" | custom-call | tf_op jit(solution)/shard_map/jit(cholesky)/cholesky | solution.py:76
  402.7 9.8 %custom-call.11 = f32[1,128,128]{1,2,0:T(8,128)S(1)} custom-call(f32[1,128,128]{2,1,0:T(8,128)S(1)} %fusion.85), custom_call_target="InvertDiagBlocksLowerTriangular" | custom-call | tf_op jit(solution)/shard_map/triangular_solve/custom-call.0 | solution.py:77
  415.0 8.4 %all-gather.2.cloned.1.call-done = bf16[1280,512]{1,0:T(8,128)(2,1)} async-done(((bf16[640,512]{1,0:T(8,128)(2,1)}), bf16[1280,512]{1,0:T(8,128)(2,1)}) %all-gather.2.cloned.1.call-update) | async-done | bytes 1310736 | tf_op jit(solution)/shard_map/all_gather | solution.py:80
  424.5 3.5 fusion.63
  428.1 1.7 fusion.62
  429.7 119.0 %all-reduce.16.cloned.1.call-done = (f32[512,512]{1,0:T(8,128)}, f32[512,256]{1,0:T(8,128)}) async-done(((f32[512,512]{1,0:T(8,128)}, f32[512,256]{1,0:T(8,128)}), (f32[512,512]{1,0:T(8,128)}, f32[512,256]{1,0:T(8,128)})) %all-reduce.16.cloned.1.call-update) | async-done | bytes 1572880 | tf_op jit(solution)/shard_map/psum | solution.py:87
  (177 shorter events, 52.4 us)
Async XLA Ops:
  7.2 3.6 copy-start.25
  7.2 3.6 copy-start.23
  7.2 5.4 all-to-all-start
  11.4 27.9 %copy-start.17 = (pred[128]{0:T(512)(128)(4,1)}, pred[128]{0:T(512)(128)(4,1)S(1)}, u32[]{:S(2)}) copy-start(pred[128]{0:T(512)(128)(4,1)S(1)} %get-tuple-element.89) | copy-start | bytes 388
  11.4 29.8 %copy-start.15 = (pred[128]{0:T(512)(128)(4,1)}, pred[128]{0:T(512)(128)(4,1)S(1)}, u32[]{:S(2)}) copy-start(pred[128]{0:T(512)(128)(4,1)S(1)} %get-tuple-element.91) | copy-start | bytes 388
  11.4 4.9 copy-start.28
  12.5 15.0 %all-to-all-start.1 = ((bf16[2,640,512]{2,1,0:T(8,128)(2,1)}), bf16[2,640,512]{2,1,0:T(8,128)(2,1)S(1)}, u32[]{:S(2)}, u32[]{:S(2)}) async-start(bf16[2,640,512]{2,1,0:T(8,128)(2,1)} %bitcast.251), calls=%async_computation.1 | async-start | bytes 2621440 | tf_op jit(solution)/shard_map/all_to_all | solution.py:27
  16.2 145.2 %all-reduce.14.cloned.1.call-start = ((), (), s32[]{:S(2)}) async-start(), calls=%async_computation.3 | async-start | bytes 2097152 | tf_op jit(solution)/shard_map/psum | solution.py:47
  21.8 3.1 copy-start.13
  21.8 3.1 copy-start.31
  21.8 3.1 copy-start.33
  22.5 9.3 %copy-start.29 = (s32[1024]{0:T(1024)}, s32[1024]{0:T(1024)S(1)}, u32[]{:S(2)}) copy-start(s32[1024]{0:T(1024)S(1)} %pad_clamp_fusion.2) | copy-start | bytes 12292
  26.9 396.5 %all-gather.2.cloned.1.call-start = ((), (), s32[]{:S(2)}) async-start(), calls=%async_computation.2 | async-start | bytes 1966080 | tf_op jit(solution)/shard_map/all_gather | solution.py:80
  95.6 91.7 %copy-start.37 = (s32[128]{0:T(128)S(1)}, s32[128]{0:T(128)}, u32[]{:S(2)}) copy-start(s32[128]{0:T(128)} %get-tuple-element.78) | copy-start | bytes 1540
  161.4 25.9 %copy-start.5 = (f32[128,512]{1,0:T(8,128)S(1)}, f32[128,512]{1,0:T(8,128)}, u32[]{:S(2)}) copy-start(f32[128,512]{1,0:T(8,128)} %get-tuple-element.63) | copy-start | bytes 786436
  239.0 23.8 %copy-start.36 = (s32[128]{0:T(128)S(1)}, s32[128]{0:T(128)}, u32[]{:S(2)}) copy-start(s32[128]{0:T(128)} %get-tuple-element.79) | copy-start | bytes 1540
  313.8 24.4 %copy-start.10 = (bf16[128,512]{1,0:T(8,128)(2,1)S(1)}, bf16[128,512]{1,0:T(8,128)(2,1)}, u32[]{:S(2)}) copy-start(bf16[128,512]{1,0:T(8,128)(2,1)} %get-tuple-element.58) | copy-start | bytes 393220
  388.8 24.0 %copy-start.35 = (s32[128]{0:T(128)S(1)}, s32[128]{0:T(128)}, u32[]{:S(2)}) copy-start(s32[128]{0:T(128)} %get-tuple-element.77) | copy-start | bytes 1540
  389.4 23.9 %copy-start.8 = (bf16[128,512]{1,0:T(8,128)(2,1)S(1)}, bf16[128,512]{1,0:T(8,128)(2,1)}, u32[]{:S(2)}) copy-start(bf16[128,512]{1,0:T(8,128)(2,1)} %get-tuple-element.56) | copy-start | bytes 393220
  413.5 10.9 %copy-start.6 = (bf16[1280,512]{1,0:T(8,128)(2,1)S(1)}, bf16[1280,512]{1,0:T(8,128)(2,1)}, u32[]{:S(2)}) copy-start(bf16[1280,512]{1,0:T(8,128)(2,1)} %param.21) | copy-start | bytes 3932164
  413.6 10.9 %copy-start.38 = (f32[1280]{0:T(1024)S(1)}, f32[1280]{0:T(1024)}, u32[]{:S(2)}) copy-start(f32[1280]{0:T(1024)} %param.22) | copy-start | bytes 15364
  414.9 133.8 %all-reduce.16.cloned.1.call-start = ((), (), s32[]{:S(2)}) async-start(), calls=%async_computation.4 | async-start | bytes 3145728 | tf_op jit(solution)/shard_map/psum | solution.py:87
  424.5 3.6 copy-start.11
  424.5 3.6 copy-start.14
  (20 other events, 32.6 us)
Sparse Core Ops, SparseCore 0:
  27.0 134.3 all-reduce.13
  415.0 8.2 all-gather.1
  429.9 118.8 all-reduce.15
where the time goes:
time: 563 us; the launch traced here: 558 us
  waiting for transfers between devices  194 us (34%)
  blocking collectives  191 us (34%)
  other arithmetic  110 us (20%)
  local copies, waits for them, and re-layouts  20.8 us (4%)
  matrix products  20.8 us (4%)
  between operations  14.9 us (3%)
  starting transfers between devices  7.27 us (1%)
    psum x4, blocking collectives, body(): lax.psum((sel_points, sel_factor, sel_built), ('rows', 'cols'))  191 us
    psum x1, waiting for transfers between devices, body(): old_full, new_full = lax.psum((old_part, new_part), 'rows')  119 us
    psum x1, waiting for transfers between devices, body(): lax.psum((sel_points, sel_factor, sel_built), ('rows', 'cols'))  65.8 us
    another operation x12, other arithmetic, body(): lower = jnp.linalg.cholesky(block)  49.6 us
    another operation x8, other arithmetic, body(): lax.linalg.triangular_solve(lower, identity, left_side=True, lower=True)  41.9 us
  transfers between devices with their start and end apart: 5, of which 4 were waited for; matrix products, arithmetic and copies ran while one was open for 5% of the time, Pallas kernels for 0%

commit v1 on v0

v1 whole, which is shorter than its diff:
```python
import functools
import math

import jax
import jax.numpy as jnp
from jax import lax
from jax.experimental import pallas as pl
from jax.experimental.pallas import tpu as pltpu
from jax.sharding import PartitionSpec as P

RIDGE_LEVEL = 1.0
BLOCK = 8
VMEM = pltpu.VMEM
HIGH = lax.Precision.HIGHEST
NT = (((1,), (1,)), ((), ()))
TN = (((0,), (0,)), ((), ()))


def inner_size(rows):
    inner = 1
    while inner * inner * 4 <= rows:
        inner *= 2
    return inner


def remote(src, dst, send, recv, row, col):
    return pltpu.make_async_remote_copy(
        src_ref=src, dst_ref=dst, send_sem=send, recv_sem=recv,
        device_id=(row, col), device_id_type=pl.DeviceIdType.MESH,
    )


def greet(me, col, inner, outer):
    place, layer = me % inner, me // inner
    barrier = pltpu.get_barrier_semaphore()
    peers = [(me, 1 - col)]
    peers += [(layer * inner + (place + d) % inner, col) for d in range(1, inner)]
    peers += [(((layer + d) % outer) * inner + place, col) for d in range(1, outer)]
    for peer in peers:
        pl.semaphore_signal(barrier, inc=1, device_id=peer, device_id_type=pl.DeviceIdType.MESH)
    pl.semaphore_wait(barrier, len(peers))


def pick_kernel(ids_ref, points_ref, factor_ref, out_ref):
    here = points_ref.shape[0]
    first = lax.axis_index("rows") * here
    ids = ids_ref[...]
    spots = lax.broadcasted_iota(jnp.int32, (ids.shape[0], here), 1) + first
    hot = jnp.where(spots == ids, 1.0, 0.0).astype(jnp.bfloat16)
    width = points_ref.shape[1]
    out_ref[:, :width] = jnp.dot(hot, points_ref[...], preferred_element_type=jnp.float32).astype(jnp.bfloat16)
    out_ref[:, width:] = jnp.dot(hot, factor_ref[...], preferred_element_type=jnp.float32).astype(jnp.bfloat16)


def pivot_kernel(inner, outer, part, points, factor, piv, other_points, other_factor,
                 buf_a, buf_b, acc, a_send, a_recv, b_send, b_recv, c_send, c_recv,
                 d_send, d_recv, e_send, e_recv, x_send, x_recv):
    me = lax.axis_index("rows")
    col = lax.axis_index("cols")
    place, layer = me % inner, me // inner
    half = other_points.shape[0]
    greet(me, col, inner, outer)
    sent = []
    stage = []
    for d in range(1, inner):
        p = (place + d) % inner
        c = remote(part.at[:, p], buf_a.at[d - 1], a_send.at[d - 1], a_recv.at[d - 1], layer * inner + p, col)
        c.start()
        stage.append(c)
    theirs = pl.ds(pl.multiple_of((1 - col) * half, 16), half)
    swap = [
        remote(points.at[theirs], other_points, x_send.at[0], x_recv.at[0], me, 1 - col),
        remote(factor.at[theirs], other_factor, x_send.at[1], x_recv.at[1], me, 1 - col),
    ]
    for c in swap:
        c.start()
    total = part[:, place]
    for c in stage:
        c.wait_recv()
    for d in range(1, inner):
        total = total + buf_a[d - 1]
    acc[...] = total
    sent += stage
    stage = []
    for d in range(1, outer):
        z = (layer + d) % outer
        c = remote(acc.at[z], buf_b.at[d - 1], b_send.at[d - 1], b_recv.at[d - 1], z * inner + place, col)
        c.start()
        stage.append(c)
    mine = acc[layer]
    for c in stage:
        c.wait_recv()
    for d in range(1, outer):
        mine = mine + buf_b[d - 1]
    piv[col, layer, place] = mine
    sent += stage
    stage = []
    for d in range(1, outer):
        z = (layer + d) % outer
        c = remote(piv.at[col, layer, place], piv.at[col, layer, place], c_send.at[d - 1], c_recv.at[d - 1],
                   z * inner + place, col)
        c.start()
        stage.append(c)
    for c in stage:
        c.wait_recv()
    sent += stage
    stage = []
    for d in range(1, inner):
        p = (place + d) % inner
        c = remote(piv.at[col, :, place], piv.at[col, :, place], d_send.at[d - 1], d_recv.at[d - 1],
                   layer * inner + p, col)
        c.start()
        stage.append(c)
    last = []
    for d in range(inner):
        p = (place + inner - d) % inner
        if d:
            stage[d - 1].wait_recv()
        c = remote(piv.at[col, :, p], piv.at[col, :, p], e_send.at[d], e_recv.at[d], me, 1 - col)
        c.start()
        last.append(c)
    sent += stage
    for c in last + swap:
        c.wait_recv()
    for c in sent + last + swap:
        c.wait_send()


def factor_block(size, a, e, rows, outs, wide):
    for first in range(0, size, BLOCK):
        span = slice(first, first + BLOCK)
        strip = a[span, :]
        for k in range(BLOCK):
            wide[k] = jnp.broadcast_to(strip[:, first + k:first + k + 1], (BLOCK, size))
        d = {(i, k): wide[k, i:i + 1, :] for i in range(BLOCK) for k in range(i + 1)}
        r = [a[first + i:first + i + 1, :] for i in range(BLOCK)]
        s = [e[first + i:first + i + 1, :] for i in range(BLOCK)]
        for k in range(BLOCK):
            scale = lax.rsqrt(d[k, k])
            r[k] = r[k] * scale
            s[k] = s[k] * scale
            for i in range(k + 1, BLOCK):
                d[i, k] = d[i, k] * scale
            for i in range(k + 1, BLOCK):
                r[i] = r[i] - d[i, k] * r[k]
                s[i] = s[i] - d[i, k] * s[k]
                for m in range(k + 1, i + 1):
                    d[i, m] = d[i, m] - d[i, k] * d[m, k]
        for k in range(BLOCK):
            rows[k:k + 1, :] = r[k]
            e[first + k:first + k + 1, :] = s[k]
        after = first + BLOCK
        if after < size:
            upper = jnp.transpose(rows[...])
            rest_a = a[after:, :]
            rest_e = e[after:, :]
            for k in range(BLOCK):
                column = upper[after:, k:k + 1]
                rest_a = rest_a - column * rows[k:k + 1, :]
                rest_e = rest_e - column * e[first + k:first + k + 1, :]
            a[after:, :] = rest_a
            e[after:, :] = rest_e


def panel_kernel(panels, ids_ref, piv, points, factor, other_points, other_factor, out_ref,
                 cols, pan, a, e, rows, wide):
    me = lax.axis_index("rows")
    col = lax.axis_index("cols")
    here, fw = points.shape
    half = here // 2
    size = cols.shape[2]
    feats, rank = 2 * fw, 2 * factor.shape[1]
    mine = pl.ds(pl.multiple_of(col * half, 16), half)
    p_self, p_other = piv.at[col], piv.at[1 - col]
    f32 = jnp.float32

    def norm(x, y):
        x, y = x.astype(f32), y.astype(f32)
        return jnp.sum(x * x, axis=1, keepdims=True) + jnp.sum(y * y, axis=1, keepdims=True)

    own_norm = norm(points[mine, :], other_points[...])
    piv_norm = norm(p_self[:, :fw], p_other[:, :fw])
    first = me * here + col * half
    own_ids = lax.broadcasted_iota(jnp.int32, (half, size), 0) + first
    place_r = lax.broadcasted_iota(jnp.int32, (panels * size, size), 0)
    place_c = lax.broadcasted_iota(jnp.int32, (panels * size, size), 1)

    def dot(x, y):
        return lax.dot_general(x, y, NT, preferred_element_type=f32)

    for q in range(panels):
        span = slice(q * size, (q + 1) * size)
        ps, po = p_self[span, :], p_other[span, :]
        row_norm = jnp.transpose(jnp.broadcast_to(piv_norm[span, :], (size, size)))[0:1, :]

        def entries(xs, xo, ys, yo, n, same):
            cross = dot(xs, ps[:, :fw]) + dot(xo, po[:, :fw])
            schur = dot(ys, ps[:, fw:]) + dot(yo, po[:, fw:])
            dist = n + row_norm - 2.0 * cross
            return jnp.exp(-dist / feats) + jnp.where(same, RIDGE_LEVEL, 0.0) + schur / (3.0 * rank)

        cols[q, :half, :] = entries(points[mine, :], other_points[...], factor[mine, :], other_factor[...],
                                    own_norm, own_ids == ids_ref[:, span])
        cols[q, half:, :] = entries(p_self[:, :fw], p_other[:, :fw], p_self[:, fw:], p_other[:, fw:],
                                    piv_norm, place_r == place_c + q * size)
    eye = jnp.where(place_r[:size, :] == place_c[:size, :], 1.0, 0.0)

    @pl.loop(0, panels)
    def _(q):
        e[...] = eye
        a[...] = cols[q, pl.ds(pl.multiple_of(half + q * size, 8), size), :]
        factor_block(size, a, e, rows, None, wide)
        pan[...] = lax.dot_general(cols[q], e[...], NT, precision=HIGH,
                                   preferred_element_type=f32).astype(jnp.bfloat16)
        out_ref[:, pl.ds(pl.multiple_of(q * size, size), size)] = pan[:half, :]
        for later in range(1, panels):
            @pl.when(later > q)
            def _():
                cols[later] = cols[later] - dot(pan[...], pan[half + later * size:half + (later + 1) * size, :])


def gram_kernel(inner, outer, scale, built, factor, weights, own_cols, gram,
                theirs, part, keep, buf_a, mid, acc, buf_b,
                a_send, a_recv, b_send, b_recv, x_send, x_recv):
    me = lax.axis_index("rows")
    col = lax.axis_index("cols")
    place, layer = me % inner, me // inner
    half, wide = built.shape
    width = own_cols.shape[1]
    rank = factor.shape[1]
    chunk = gram.shape[0]
    f32 = jnp.float32
    greet(me, col, inner, outer)
    swap = remote(built, theirs, x_send, x_recv, me, 1 - col)
    swap.start()
    lanes = pl.ds(pl.multiple_of(col * width, 128), width)

    def add(source, which, start):
        span = pl.ds(pl.multiple_of(which * half, 16), half)
        weighted = (source[...].astype(f32) * weights[span, :]).astype(jnp.bfloat16)
        own = source[:, lanes]
        own_cols[span, :] = own
        old = lax.dot_general(weighted, factor[span, :], TN, preferred_element_type=f32)
        new = lax.dot_general(weighted, own, TN, preferred_element_type=f32)
        if start:
            keep[:, :rank] = old
            keep[:, rank:] = new
        else:
            keep[:, :rank] = (keep[:, :rank] + old) * scale
            keep[:, rank:] = (keep[:, rank:] + new) * scale

    add(built, col, True)
    swap.wait_recv()
    add(theirs, 1 - col, False)
    for z in range(outer):
        for p in range(inner):
            first = (z * inner + p) * chunk
            part[z, p] = keep[first:first + chunk, :].astype(jnp.bfloat16)
    stage = []
    for d in range(1, inner):
        p = (place + d) % inner
        c = remote(part.at[:, p], buf_a.at[d - 1], a_send.at[d - 1], a_recv.at[d - 1], layer * inner + p, col)
        c.start()
        stage.append(c)
    for z in range(outer):
        acc[z] = keep[pl.ds(pl.multiple_of((z * inner + place) * chunk, 8), chunk), :]
    for d in range(1, inner):
        stage[d - 1].wait_recv()
        acc[...] = acc[...] + buf_a[d - 1].astype(f32)
    mid[...] = acc[...].astype(jnp.bfloat16)
    second = []
    for d in range(1, outer):
        z = (layer + d) % outer
        c = remote(mid.at[z], buf_b.at[d - 1], b_send.at[d - 1], b_recv.at[d - 1], z * inner + place, col)
        c.start()
        second.append(c)
    total = acc[layer]
    for d in range(1, outer):
        second[d - 1].wait_recv()
        total = total + buf_b[d - 1].astype(f32)
    gram[...] = total
    for c in stage + second + [swap]:
        c.wait_send()


def body(points, factor, weights, pivot_slots, pivot_owners):
    here, fw = points.shape
    rank = factor.shape[1]
    panels, size = pivot_slots.shape
    rows = lax.axis_size("rows")
    inner = inner_size(rows)
    outer = rows // inner
    count = panels * size
    chunk = count // rows
    width = fw + rank
    half = here // 2
    bf16, f32 = jnp.bfloat16, jnp.float32
    ids = (pivot_owners * here + pivot_slots).reshape(count)
    vm = pl.BlockSpec(memory_space=VMEM)
    sem = lambda n: pltpu.SemaphoreType.DMA((n,))
    limit = 60 * 1024 * 1024

    part = pl.pallas_call(
        pick_kernel,
        out_shape=jax.ShapeDtypeStruct((count, width), bf16),
        in_specs=[vm] * 3, out_specs=vm, name="pick",
        compiler_params=pltpu.CompilerParams(vmem_limit_bytes=limit),
    )(ids[:, None], points, factor)

    piv, other_points, other_factor = pl.pallas_call(
        functools.partial(pivot_kernel, inner, outer),
        out_shape=(
            jax.ShapeDtypeStruct((2, outer, inner, chunk, width), bf16),
            jax.ShapeDtypeStruct((half, fw), bf16),
            jax.ShapeDtypeStruct((half, rank), bf16),
        ),
        in_specs=[vm] * 3, out_specs=(vm,) * 3, name="pivots",
        scratch_shapes=[
            VMEM((inner - 1, outer, chunk, width), bf16),
            VMEM((outer - 1, chunk, width), bf16),
            VMEM((outer, chunk, width), bf16),
            sem(inner - 1), sem(inner - 1), sem(outer - 1), sem(outer - 1),
            sem(outer - 1), sem(outer - 1), sem(inner - 1), sem(inner - 1),
            sem(inner), sem(inner), sem(2), sem(2),
        ],
        compiler_params=pltpu.CompilerParams(collective_id=0, has_side_effects=True, vmem_limit_bytes=limit),
    )(part.reshape(outer, inner, chunk, width), points, factor)

    built = pl.pallas_call(
        functools.partial(panel_kernel, panels),
        out_shape=jax.ShapeDtypeStruct((half, count), bf16),
        in_specs=[vm] * 6, out_specs=vm, name="panels",
        scratch_shapes=[
            VMEM((panels, half + count, size), f32),
            VMEM((half + count, size), bf16),
            VMEM((size, size), f32), VMEM((size, size), f32),
            VMEM((BLOCK, size), f32), VMEM((BLOCK, BLOCK, size), f32),
        ],
        compiler_params=pltpu.CompilerParams(vmem_limit_bytes=limit),
    )(ids[None, :], piv.reshape(2, count, width), points, factor, other_points, other_factor)

    scale = size / math.sqrt(here * rows)
    gw = rank + count // 2
    own_cols, gram = pl.pallas_call(
        functools.partial(gram_kernel, inner, outer, scale),
        out_shape=(
            jax.ShapeDtypeStruct((here, count // 2), bf16),
            jax.ShapeDtypeStruct((chunk, gw), f32),
        ),
        in_specs=[vm] * 3, out_specs=(vm,) * 2, name="gram",
        scratch_shapes=[
            VMEM((half, count), bf16),
            VMEM((outer, inner, chunk, gw), bf16),
            VMEM((count, gw), f32),
            VMEM((inner - 1, outer, chunk, gw), bf16),
            VMEM((outer, chunk, gw), bf16),
            VMEM((outer, chunk, gw), f32),
            VMEM((outer - 1, chunk, gw), bf16),
            sem(inner - 1), sem(inner - 1), sem(outer - 1), sem(outer - 1),
            pltpu.SemaphoreType.DMA, pltpu.SemaphoreType.DMA,
        ],
        compiler_params=pltpu.CompilerParams(collective_id=1, has_side_effects=True, vmem_limit_bytes=limit),
    )(built, factor, weights[:, None])
    return own_cols, gram[:, :rank], gram[:, rank:]


def solution(mesh):
    return jax.shard_map(
        body,
        mesh=mesh,
        in_specs=(P("rows", "cols"), P("rows", "cols"), P("rows"), P(), P()),
        out_specs=(P("rows", "cols"), P("rows", "cols"), P("rows", "cols")),
        check_vma=False,
    )
```

time: 563 us -> 107 us (0.19)
  waiting for transfers between devices: 194 us -> 0 us
  blocking collectives: 191 us -> 0 us
  other arithmetic: 110 us -> 0.7 us
  Pallas kernels: 0 us -> 98.5 us
  matrix products: 20.8 us -> 0 us
  between operations: 14.9 us -> 0.66 us
  local copies, waits for them, and re-layouts: 20.8 us -> 6.75 us
  starting transfers between devices: 7.27 us -> 0 us
    psum x4 -> x0, blocking collectives: 191 us -> none  [body(): lax.psum((sel_points, sel_factor, sel_built), ('rows', 'cols'))]
    psum x2 -> x0, waiting for transfers between devices: 185 us -> none  [the longest x1 119 us: body(): old_full, new_full = lax.psum((old_part, new_part), 'rows')]
    pallas_call x0 -> x4, Pallas kernels: none -> 98.5 us  [the longest x1 38.1 us: body(): pl.pallas_call(functools.partial(pivot_kernel, inner, outer), out_shape=(...]
    another operation x23 -> x0, other arithmetic: 93.5 us -> none  [the longest x12 49.6 us: body(): lower = jnp.linalg.cholesky(block)]
    dot_general x30 -> x0, matrix products: 19.6 us -> none  [the longest x4 3.85 us: body(): jnp.dot(columns, inverse.T, precision=lax.Precision.HIGHEST)]
    gather x12 -> x0, local copies, waits for them, and re-layouts: 14.6 us -> none  [the longest x4 6.06 us: body(): jnp.take(full_factor, local_slots, axis=0).astype(jnp.float32)]
    select_n x10 -> x0, other arithmetic: 9.65 us -> none  [the longest x4 5.9 us: body(): jnp.where(chosen, jnp.take(full_factor, local_slots, axis=0).astype(jnp.f...]
    all_gather x1 -> x0, waiting for transfers between devices: 8.39 us -> none  [body(): built = lax.all_gather(built_half, 'cols', axis=0, tiled=True)]
  transfers between devices with their start and end apart: 5 -> 0, of which waited for: 4 -> 0; matrix products, arithmetic and copies ran while one was open for 5% -> 0% of each run, Pallas kernels for 0% -> 0%
where the time goes in v1:
time: 107 us
  Pallas kernels  98.5 us (92%)
  local copies, waits for them, and re-layouts  6.75 us (6%)
    pallas_call x1, Pallas kernels, body(): pl.pallas_call(functools.partial(pivot_kernel, inner, outer), out_shape=(...  38.1 us
    pallas_call x1, Pallas kernels, body(): pl.pallas_call(functools.partial(panel_kernel, panels), out_shape=jax.Sha...  32.1 us
    pallas_call x1, Pallas kernels, body(): pl.pallas_call(functools.partial(gram_kernel, inner, outer, scale), out_s...  24.6 us
    pallas_call x1, Pallas kernels, body(): pl.pallas_call(pick_kernel, out_shape=jax.ShapeDtypeStruct((count, width)...  3.74 us
    slice x2, local copies, waits for them, and re-layouts, body(): return (own_cols, gram[:, :rank], gram[:, rank:])  2.85 us

profile of v1, /device:TPU:0, one launch (start us, length us, event | category | flops | bytes accessed | tf_op | source)
XLA Modules:
  0.0 106.6 jit_solution(16093829631378267690)
XLA Ops:
  0.6 0.7 multiply_add_fusion
  1.3 0.0 copy-start
  1.3 0.9 copy.8.ids_ref
  2.2 3.7 %pick.1 = bf16[512,768]{1,0:T(8,128)(2,1)} custom-call(s32[512,1]{1,0:T(8,128)} %copy.8.ids_ref, bf16[1280,256]{1,0:T(8,128)(2,1)} %points.3, bf16[1280,512]{1,0:T(8,128)(2,1)} %factor.5), custom_call_target="tpu_custom_call" | custom-call | tf_op jit(solution)/shard_map/pick/pallas_call | solution.py:303
  5.9 0.0 copy-done
  5.9 38.1 %pivots.1 = (bf16[2,4,4,32,768]{4,3,2,1,0:T(8,128)(2,1)}, bf16[640,256]{1,0:T(8,128)(2,1)}, bf16[640,512]{1,0:T(8,128)(2,1)}) custom-call(bf16[4,4,32,768]{3,2,1,0:T(8,128)(2,1)} %bitcast.4, bf16[1280,256]{1,0:T(8,128)(2,1)} %points.3, bf16[1280,512]{1,0:T(8,128)(2,1)} %factor.5), custom_call_target="tpu_custom_call" | custom-call | tf_op jit(solution)/shard_map/pivots/pallas_call | solution.py:310
  44.0 0.0 copy-start.1
  44.0 32.1 %panels.1.built = bf16[640,512]{1,0:T(8,128)(2,1)} custom-call(s32[1,512]{1,0:T(1,128)} %bitcast.7, bf16[2,512,768]{2,1,0:T(8,128)(2,1)} %bitcast.5, bf16[1280,256]{1,0:T(8,128)(2,1)} %points.3, bf16[1280,512]{1,0:T(8,128)(2,1)} %factor.5, bf16[640,256]{1,0:T(8,128)(2,1)} %get-tuple-element.9.other_points, bf16[640,512]{1,0:T(8,128)(2,1)} %get-tuple-element.10.other_factor), custom_call_target="tpu_custom_call" | custom-call | tf_op jit(solution)/shard_map/panels/pallas_call | solution.py:329
  76.1 0.0 copy-done.1
  76.1 1.1 %broadcast_in_dim.4.weights = f32[1280,1]{1,0:T(8,128)} reshape(f32[1280]{0:T(1024)S(1)} %copy-done.1) | data formatting | bytes 10240 | tf_op jit(solution)/shard_map/broadcast_in_dim | solution.py:363
  77.2 24.6 %gram.1 = (bf16[1280,256]{1,0:T(8,128)(2,1)}, f32[32,768]{1,0:T(8,128)}) custom-call(bf16[640,512]{1,0:T(8,128)(2,1)} %panels.1.built, bf16[1280,512]{1,0:T(8,128)(2,1)} %factor.5, f32[1280,1]{1,0:T(8,128)} %broadcast_in_dim.4.weights), custom_call_target="tpu_custom_call" | custom-call | tf_op jit(solution)/shard_map/gram/pallas_call | solution.py:344
  101.8 1.5 %slice.6 = f32[32,512]{1,0:T(8,128)} slice(f32[32,768]{1,0:T(8,128)} %get-tuple-element.12), slice={[0:32], [0:512]} | slice | bytes 131072 | tf_op jit(solution)/shard_map/slice | solution.py:364
  103.3 1.4 %slice.7 = f32[32,256]{1,0:T(8,128)} slice(f32[32,768]{1,0:T(8,128)} %get-tuple-element.12), slice={[0:32], [512:768]} | slice | bytes 65536 | tf_op jit(solution)/shard_map/slice | solution.py:364
  104.7 2.0 %copy.11 = bf16[1280,256]{1,0:T(8,128)(2,1)} copy(bf16[1280,256]{1,0:T(8,128)(2,1)} %get-tuple-element.16) | data formatting | bytes 1310720
Async XLA Ops:
  1.3 4.6 %copy-start = (s32[4,128]{1,0:T(4,128)}, s32[4,128]{1,0:T(4,128)S(1)}, u32[]{:S(2)}) copy-start(s32[4,128]{1,0:T(4,128)S(1)} %multiply_add_fusion) | copy-start | bytes 6148
  44.0 32.1 %copy-start.1 = (f32[1280]{0:T(1024)S(1)}, f32[1280]{0:T(1024)}, u32[]{:S(2)}) copy-start(f32[1280]{0:T(1024)} %param.7) | copy-start | bytes 15364

commit v2 on v1

v2 whole, which is shorter than its diff:
```python
import functools
import math

import jax
import jax.numpy as jnp
from jax import lax
from jax.experimental import pallas as pl
from jax.experimental.pallas import tpu as pltpu
from jax.sharding import PartitionSpec as P

RIDGE_LEVEL = 1.0
BLOCK = 8
VMEM = pltpu.VMEM
HIGH = lax.Precision.HIGHEST
NT = (((1,), (1,)), ((), ()))
TN = (((0,), (0,)), ((), ()))


def inner_size(rows):
    inner = 1
    while inner * inner * 4 <= rows:
        inner *= 2
    return inner


def remote(src, dst, send, recv, row, col):
    return pltpu.make_async_remote_copy(
        src_ref=src, dst_ref=dst, send_sem=send, recv_sem=recv,
        device_id=(row, col), device_id_type=pl.DeviceIdType.MESH,
    )


def greet(me, col, inner, outer):
    place, layer = me % inner, me // inner
    barrier = pltpu.get_barrier_semaphore()
    peers = [(me, 1 - col)]
    peers += [(layer * inner + (place + d) % inner, col) for d in range(1, inner)]
    peers += [(((layer + d) % outer) * inner + place, col) for d in range(1, outer)]
    for peer in peers:
        pl.semaphore_signal(barrier, inc=1, device_id=peer, device_id_type=pl.DeviceIdType.MESH)
    pl.semaphore_wait(barrier, len(peers))


def factor_block(size, a, e, rows, outs, wide):
    for first in range(0, size, BLOCK):
        span = slice(first, first + BLOCK)
        strip = a[span, :]
        for k in range(BLOCK):
            wide[k] = jnp.broadcast_to(strip[:, first + k:first + k + 1], (BLOCK, size))
        d = {(i, k): wide[k, i:i + 1, :] for i in range(BLOCK) for k in range(i + 1)}
        r = [a[first + i:first + i + 1, :] for i in range(BLOCK)]
        s = [e[first + i:first + i + 1, :] for i in range(BLOCK)]
        for k in range(BLOCK):
            scale = lax.rsqrt(d[k, k])
            r[k] = r[k] * scale
            s[k] = s[k] * scale
            for i in range(k + 1, BLOCK):
                d[i, k] = d[i, k] * scale
            for i in range(k + 1, BLOCK):
                r[i] = r[i] - d[i, k] * r[k]
                s[i] = s[i] - d[i, k] * s[k]
                for m in range(k + 1, i + 1):
                    d[i, m] = d[i, m] - d[i, k] * d[m, k]
        for k in range(BLOCK):
            rows[k:k + 1, :] = r[k]
            e[first + k:first + k + 1, :] = s[k]
        after = first + BLOCK
        if after < size:
            upper = jnp.transpose(rows[...])
            rest_a = a[after:, :]
            rest_e = e[after:, :]
            for k in range(BLOCK):
                column = upper[after:, k:k + 1]
                rest_a = rest_a - column * rows[k:k + 1, :]
                rest_e = rest_e - column * e[first + k:first + k + 1, :]
            a[after:, :] = rest_a
            e[after:, :] = rest_e


def panel_kernel(inner, outer, slots, owners, points, factor, out_ref,
                 part, piv, other_points, other_factor, buf_a, buf_b, acc,
                 prow, inv, norms, a, rows, wide,
                 a_send, a_recv, b_send, b_recv, c_send, c_recv,
                 d_send, d_recv, e_send, e_recv, x_send, x_recv):
    me = lax.axis_index("rows")
    col = lax.axis_index("cols")
    place, layer = me % inner, me // inner
    panels, size = slots.shape
    here, fw = points.shape
    half = here // 2
    feats, rank = 2 * fw, 2 * factor.shape[1]
    chunk = size // inner
    f32, bf16 = jnp.float32, jnp.bfloat16
    greet(me, col, inner, outer)

    def piece(q, p):
        return pl.ds(pl.multiple_of(q * size + p * chunk, chunk), chunk)

    def turned(row):
        return jnp.transpose(jnp.broadcast_to(row, (size, size)))

    spots = lax.broadcasted_iota(jnp.int32, (size, here), 1) + me * here
    step_a = []
    for q in range(panels):
        ids = (owners[q:q + 1, :] * here + slots[q:q + 1, :]).astype(f32)
        hot = jnp.where(spots == turned(ids)[:, 0:1].astype(jnp.int32), 1.0, 0.0).astype(bf16)
        span = slice(q * size, (q + 1) * size)
        part[span, :fw] = jnp.dot(hot, points[...], preferred_element_type=f32).astype(bf16)
        part[span, fw:] = jnp.dot(hot, factor[...], preferred_element_type=f32).astype(bf16)
        for d in range(1, inner):
            p = (place + d) % inner
            c = remote(part.at[piece(q, p)], buf_a.at[q, d - 1], a_send.at[q, d - 1], a_recv.at[q, d - 1],
                       layer * inner + p, col)
            c.start()
            step_a.append(c)
    theirs = pl.ds(pl.multiple_of((1 - col) * half, 16), half)
    swap = [
        remote(points.at[theirs], other_points, x_send.at[0], x_recv.at[0], me, 1 - col),
        remote(factor.at[theirs], other_factor, x_send.at[1], x_recv.at[1], me, 1 - col),
    ]
    for c in swap:
        c.start()

    def to_owner(q):
        return remote(acc.at[q], buf_b.at[layer], b_send.at[q], b_recv.at[layer], q * inner + place, col)

    def from_layer(z):
        return remote(acc.at[0], buf_b.at[z], b_send.at[0], b_recv.at[z], z * inner + place, col)

    def spread(q, z):
        here_it = piv.at[col, piece(q, place)]
        return remote(here_it, here_it, c_send.at[z], c_recv.at[q], z * inner + place, col)

    def around(q, d):
        it = piv.at[col, piece(q, place)]
        return remote(it, it, d_send.at[q, d - 1], d_recv.at[q, d - 1], layer * inner + (place + d) % inner, col)

    def across(q, d):
        it = piv.at[col, piece(q, (place + inner - d) % inner)]
        return remote(it, it, e_send.at[q, d], e_recv.at[q, d], me, 1 - col)

    def collect(q):
        @pl.when(layer == q)
        def _():
            mine = acc[q]
            for d in range(1, outer):
                z = (q + d) % outer
                from_layer(z).wait_recv()
                mine = mine + buf_b[z]
            piv[col, piece(q, place)] = mine
            for d in range(1, outer):
                spread(q, (q + d) % outer).start()

    for q in range(panels):
        total = part[piece(q, place), :]
        for d in range(1, inner):
            step_a[q * (inner - 1) + d - 1].wait_recv()
            total = total + buf_a[q, d - 1]
        acc[q] = total

        @pl.when(layer != q)
        def _():
            to_owner(q).start()
        if q:
            collect(q - 1)
    collect(panels - 1)
    for q in range(panels):
        @pl.when(layer != q)
        def _():
            spread(q, layer).wait_recv()
        for d in range(1, inner):
            around(q, d).start()
        across(q, 0).start()

    def forward(q):
        for d in range(1, inner):
            around(q, d).wait_recv()
            across(q, d).start()

    forward(0)
    prow[...] = jnp.zeros_like(prow)
    out_ref[...] = jnp.zeros_like(out_ref)
    for c in swap:
        c.wait_recv()

    def norm(x, y):
        x, y = x.astype(f32), y.astype(f32)
        return jnp.sum(x * x, axis=1, keepdims=True) + jnp.sum(y * y, axis=1, keepdims=True)

    def dot(x, y):
        return lax.dot_general(x, y, NT, preferred_element_type=f32)

    mine = pl.ds(pl.multiple_of(col * half, 16), half)
    own_norm = norm(points[mine, :], other_points[...])
    own_ids = lax.broadcasted_iota(jnp.int32, (half, size), 0) + (me * here + col * half)
    same = lax.broadcasted_iota(jnp.int32, (size, size), 0) == lax.broadcasted_iota(jnp.int32, (size, size), 1)
    eye = jnp.where(same, 1.0, 0.0)

    def panel(q, carry):
        @pl.when(q + 1 < panels)
        def _():
            forward(q + 1)
        for d in range(inner):
            across(q, d).wait_recv()
        span = pl.ds(pl.multiple_of(q * size, size), size)
        ps, po = piv[col, span, :], piv[1 - col, span, :]
        pnorm = norm(ps[:, :fw], po[:, :fw])
        norms[q] = jnp.transpose(jnp.broadcast_to(pnorm, (size, size)))

        def entries(xs, xo, ys, yo, ts, to, n, row_norm):
            cross = dot(xs, ts[:, :fw]) + dot(xo, to[:, :fw])
            schur = dot(ys, ts[:, fw:]) + dot(yo, to[:, fw:])
            return jnp.exp(-(n + row_norm - 2.0 * cross) / feats) + schur / (3.0 * rank)

        def earlier(k, carry):
            other = pl.ds(pl.multiple_of(k * size, size), size)
            ts, to = piv[col, other, :], piv[1 - col, other, :]
            row_norm = norms[k][0:1, :]
            m = entries(ps[:, :fw], po[:, :fw], ps[:, fw:], po[:, fw:], ts, to, pnorm, row_norm)
            m = m - dot(prow[q], prow[k])
            prow[q, :, other] = lax.dot_general(m, inv[k], NT, precision=HIGH,
                                                preferred_element_type=f32).astype(bf16)
            return carry

        lax.fori_loop(0, q, earlier, 0)
        row_norm = norms[q][0:1, :]
        a[...] = (entries(ps[:, :fw], po[:, :fw], ps[:, fw:], po[:, fw:], ps, po, pnorm, row_norm)
                  + RIDGE_LEVEL * eye - dot(prow[q], prow[q]))
        e = inv.at[q]
        e[...] = eye
        ids = owners[pl.ds(q, 1), :] * here + slots[pl.ds(q, 1), :]
        columns = (entries(points[mine, :], other_points[...], factor[mine, :], other_factor[...], ps, po,
                           own_norm, row_norm)
                   + jnp.where(own_ids == ids, RIDGE_LEVEL, 0.0) - dot(out_ref[...], prow[q]))
        factor_block(size, a, e, rows, None, wide)
        out_ref[:, span] = lax.dot_general(columns, e[...], NT, precision=HIGH,
                                           preferred_element_type=f32).astype(bf16)
        return carry

    lax.fori_loop(0, panels, panel, 0)
    for c in step_a + swap:
        c.wait_send()
    for q in range(panels):
        @pl.when(layer != q)
        def _():
            to_owner(q).wait_send()

        @pl.when(layer == q)
        def _():
            for d in range(1, outer):
                spread(q, (q + d) % outer).wait_send()
        for d in range(1, inner):
            around(q, d).wait_send()
        for d in range(inner):
            across(q, d).wait_send()


def gram_kernel(inner, outer, scale, built, factor, weights, own_cols, gram,
                theirs, part, keep, buf_a, mid, acc, buf_b,
                a_send, a_recv, b_send, b_recv, x_send, x_recv):
    me = lax.axis_index("rows")
    col = lax.axis_index("cols")
    place, layer = me % inner, me // inner
    half, wide = built.shape
    width = own_cols.shape[1]
    rank = factor.shape[1]
    chunk = gram.shape[0]
    f32 = jnp.float32
    greet(me, col, inner, outer)
    swap = remote(built, theirs, x_send, x_recv, me, 1 - col)
    swap.start()
    lanes = pl.ds(pl.multiple_of(col * width, 128), width)

    def add(source, which, start):
        span = pl.ds(pl.multiple_of(which * half, 16), half)
        weighted = (source[...].astype(f32) * weights[span, :]).astype(jnp.bfloat16)
        own = source[:, lanes]
        own_cols[span, :] = own
        old = lax.dot_general(weighted, factor[span, :], TN, preferred_element_type=f32)
        new = lax.dot_general(weighted, own, TN, preferred_element_type=f32)
        if start:
            keep[:, :rank] = old
            keep[:, rank:] = new
        else:
            keep[:, :rank] = (keep[:, :rank] + old) * scale
            keep[:, rank:] = (keep[:, rank:] + new) * scale

    add(built, col, True)
    swap.wait_recv()
    add(theirs, 1 - col, False)
    for z in range(outer):
        for p in range(inner):
            first = (z * inner + p) * chunk
            part[z, p] = keep[first:first + chunk, :].astype(jnp.bfloat16)
    stage = []
    for d in range(1, inner):
        p = (place + d) % inner
        c = remote(part.at[:, p], buf_a.at[d - 1], a_send.at[d - 1], a_recv.at[d - 1], layer * inner + p, col)
        c.start()
        stage.append(c)
    for z in range(outer):
        acc[z] = keep[pl.ds(pl.multiple_of((z * inner + place) * chunk, 8), chunk), :]
    for d in range(1, inner):
        stage[d - 1].wait_recv()
        acc[...] = acc[...] + buf_a[d - 1].astype(f32)
    mid[...] = acc[...].astype(jnp.bfloat16)
    second = []
    for d in range(1, outer):
        z = (layer + d) % outer
        c = remote(mid.at[z], buf_b.at[d - 1], b_send.at[d - 1], b_recv.at[d - 1], z * inner + place, col)
        c.start()
        second.append(c)
    total = acc[layer]
    for d in range(1, outer):
        second[d - 1].wait_recv()
        total = total + buf_b[d - 1].astype(f32)
    gram[...] = total
    for c in stage + second + [swap]:
        c.wait_send()


def body(points, factor, weights, pivot_slots, pivot_owners):
    here, fw = points.shape
    rank = factor.shape[1]
    panels, size = pivot_slots.shape
    rows = lax.axis_size("rows")
    inner = inner_size(rows)
    outer = rows // inner
    count = panels * size
    chunk = count // rows
    width = fw + rank
    half = here // 2
    bf16, f32 = jnp.bfloat16, jnp.float32
    vm = pl.BlockSpec(memory_space=VMEM)
    sem = lambda *n: pltpu.SemaphoreType.DMA(n)
    limit = 60 * 1024 * 1024

    split = 4 if rows % 16 == 0 else inner
    layers = rows // split
    piece = size // split
    built = pl.pallas_call(
        functools.partial(panel_kernel, split, layers),
        out_shape=jax.ShapeDtypeStruct((half, count), bf16),
        in_specs=[vm] * 4, out_specs=vm, name="panels",
        scratch_shapes=[
            VMEM((count, width), bf16), VMEM((2, count, width), bf16),
            VMEM((half, fw), bf16), VMEM((half, rank), bf16),
            VMEM((panels, split - 1, piece, width), bf16),
            VMEM((layers, piece, width), bf16),
            VMEM((panels, piece, width), bf16),
            VMEM((panels, size, count), bf16),
            VMEM((panels, size, size), f32), VMEM((panels, size, size), f32), VMEM((size, size), f32),
            VMEM((BLOCK, size), f32), VMEM((BLOCK, BLOCK, size), f32),
            sem(panels, split - 1), sem(panels, split - 1), sem(panels), sem(layers),
            sem(layers), sem(panels), sem(panels, split - 1), sem(panels, split - 1),
            sem(panels, split), sem(panels, split), sem(2), sem(2),
        ],
        compiler_params=pltpu.CompilerParams(collective_id=0, has_side_effects=True, vmem_limit_bytes=limit),
    )(pivot_slots, pivot_owners, points, factor)

    scale = size / math.sqrt(here * rows)
    gw = rank + count // 2
    own_cols, gram = pl.pallas_call(
        functools.partial(gram_kernel, inner, outer, scale),
        out_shape=(
            jax.ShapeDtypeStruct((here, count // 2), bf16),
            jax.ShapeDtypeStruct((chunk, gw), f32),
        ),
        in_specs=[vm] * 3, out_specs=(vm,) * 2, name="gram",
        scratch_shapes=[
            VMEM((half, count), bf16),
            VMEM((outer, inner, chunk, gw), bf16),
            VMEM((count, gw), f32),
            VMEM((inner - 1, outer, chunk, gw), bf16),
            VMEM((outer, chunk, gw), bf16),
            VMEM((outer, chunk, gw), f32),
            VMEM((outer - 1, chunk, gw), bf16),
            sem(inner - 1), sem(inner - 1), sem(outer - 1), sem(outer - 1),
            pltpu.SemaphoreType.DMA, pltpu.SemaphoreType.DMA,
        ],
        compiler_params=pltpu.CompilerParams(collective_id=1, has_side_effects=True, vmem_limit_bytes=limit),
    )(built, factor, weights[:, None])
    return own_cols, gram[:, :rank], gram[:, rank:]


def solution(mesh):
    return jax.shard_map(
        body,
        mesh=mesh,
        in_specs=(P("rows", "cols"), P("rows", "cols"), P("rows"), P(), P()),
        out_specs=(P("rows", "cols"), P("rows", "cols"), P("rows", "cols")),
        check_vma=False,
    )
```

time: 107 us -> 93.1 us (0.87)
  Pallas kernels: 98.5 us -> 86.2 us
    pallas_call x3 -> x1, Pallas kernels: 73.9 us -> 60.9 us  [body(): pl.pallas_call(functools.partial(panel_kernel, split, layers), out_shape=...]
where the time goes in v2:
time: 93.1 us; the launch traced here: 92.7 us
  Pallas kernels  86.2 us (93%)
  local copies, waits for them, and re-layouts  5.89 us (6%)
    pallas_call x1, Pallas kernels, body(): pl.pallas_call(functools.partial(panel_kernel, split, layers), out_shape=...  60.9 us
    pallas_call x1, Pallas kernels, body(): pl.pallas_call(functools.partial(gram_kernel, inner, outer, scale), out_s...  25.3 us
    slice x2, local copies, waits for them, and re-layouts, body(): return (own_cols, gram[:, :rank], gram[:, rank:])  2.85 us
    unnamed x3, local copies, waits for them, and re-layouts  1.97 us

profile of v2, /device:TPU:0, one launch (start us, length us, event | category | flops | bytes accessed | tf_op | source)
XLA Modules:
  0.0 92.7 jit_solution(3801476347674387802)
XLA Ops:
  0.6 0.0 copy-start
  0.6 60.9 %panels.1.built = bf16[640,512]{1,0:T(8,128)(2,1)} custom-call(s32[4,128]{1,0:T(4,128)} %slots.1, s32[4,128]{1,0:T(4,128)} %owners.1, bf16[1280,256]{1,0:T(8,128)(2,1)} %points.1, bf16[1280,512]{1,0:T(8,128)(2,1)} %factor.3), custom_call_target="tpu_custom_call" | custom-call | tf_op jit(solution)/shard_map/panels/pallas_call | solution.py:341
  61.5 0.0 copy-done
  61.5 1.1 %broadcast_in_dim.4.weights = f32[1280,1]{1,0:T(8,128)} reshape(f32[1280]{0:T(1024)S(1)} %copy-done) | data formatting | bytes 10240 | tf_op jit(solution)/shard_map/broadcast_in_dim | solution.py:382
  62.6 25.3 %gram.1 = (bf16[1280,256]{1,0:T(8,128)(2,1)}, f32[32,768]{1,0:T(8,128)}) custom-call(bf16[640,512]{1,0:T(8,128)(2,1)} %panels.1.built, bf16[1280,512]{1,0:T(8,128)(2,1)} %factor.3, f32[1280,1]{1,0:T(8,128)} %broadcast_in_dim.4.weights), custom_call_target="tpu_custom_call" | custom-call | tf_op jit(solution)/shard_map/gram/pallas_call | solution.py:363
  87.9 1.4 %slice.7 = f32[32,256]{1,0:T(8,128)} slice(f32[32,768]{1,0:T(8,128)} %get-tuple-element.6), slice={[0:32], [512:768]} | slice | bytes 65536 | tf_op jit(solution)/shard_map/slice | solution.py:383
  89.3 1.5 %slice.6 = f32[32,512]{1,0:T(8,128)} slice(f32[32,768]{1,0:T(8,128)} %get-tuple-element.6), slice={[0:32], [0:512]} | slice | bytes 131072 | tf_op jit(solution)/shard_map/slice | solution.py:383
  90.7 2.0 %copy.10 = bf16[1280,256]{1,0:T(8,128)(2,1)} copy(bf16[1280,256]{1,0:T(8,128)(2,1)} %get-tuple-element.10) | data formatting | bytes 1310720
Async XLA Ops:
  0.6 60.9 %copy-start = (f32[1280]{0:T(1024)S(1)}, f32[1280]{0:T(1024)}, u32[]{:S(2)}) copy-start(f32[1280]{0:T(1024)} %param.7) | copy-start | bytes 15364

commit v3 on v2

--- a/solution.py
+++ b/solution.py
@@ -77,10 +77,10 @@
             e[after:, :] = rest_e
 
 
-def panel_kernel(inner, outer, slots, owners, points, factor, out_ref,
+def panel_kernel(inner, outer, slots, owners, points, factor, out_ref, other_ref,
                  part, piv, other_points, other_factor, buf_a, buf_b, acc,
                  prow, inv, norms, a, rows, wide,
-                 a_send, a_recv, b_send, b_recv, c_send, c_recv,
+                 a_send, a_recv, b_send, b_recv, f_send, f_recv,
                  d_send, d_recv, e_send, e_recv, x_send, x_recv):
     me = lax.axis_index("rows")
     col = lax.axis_index("cols")
@@ -121,15 +121,9 @@
     for c in swap:
         c.start()
 
-    def to_owner(q):
-        return remote(acc.at[q], buf_b.at[layer], b_send.at[q], b_recv.at[layer], q * inner + place, col)
-
-    def from_layer(z):
-        return remote(acc.at[0], buf_b.at[z], b_send.at[0], b_recv.at[z], z * inner + place, col)
-
-    def spread(q, z):
-        here_it = piv.at[col, piece(q, place)]
-        return remote(here_it, here_it, c_send.at[z], c_recv.at[q], z * inner + place, col)
+    def along(q, d):
+        return remote(acc.at[q], buf_b.at[q, d - 1], b_send.at[q, d - 1], b_recv.at[q, d - 1],
+                      ((layer + d) % outer) * inner + place, col)
 
     def around(q, d):
         it = piv.at[col, piece(q, place)]
@@ -139,35 +133,25 @@
         it = piv.at[col, piece(q, (place + inner - d) % inner)]
         return remote(it, it, e_send.at[q, d], e_recv.at[q, d], me, 1 - col)
 
-    def collect(q):
-        @pl.when(layer == q)
-        def _():
-            mine = acc[q]
-            for d in range(1, outer):
-                z = (q + d) % outer
-                from_layer(z).wait_recv()
-                mine = mine + buf_b[z]
-            piv[col, piece(q, place)] = mine
-            for d in range(1, outer):
-                spread(q, (q + d) % outer).start()
-
-    for q in range(panels):
+    def swap_panel(q):
+        span = pl.ds(pl.multiple_of(q * size, size), size)
+        return remote(out_ref.at[:, span], other_ref.at[:, span], f_send.at[q], f_recv.at[q], me, 1 - col)
+
+    def layer_sum(q):
         total = part[piece(q, place), :]
         for d in range(1, inner):
             step_a[q * (inner - 1) + d - 1].wait_recv()
             total = total + buf_a[q, d - 1]
         acc[q] = total
-
-        @pl.when(layer != q)
-        def _():
-            to_owner(q).start()
-        if q:
-            collect(q - 1)
-    collect(panels - 1)
-    for q in range(panels):
-        @pl.when(layer != q)
-        def _():
-            spread(q, layer).wait_recv()
+        for d in range(1, outer):
+            along(q, d).start()
+
+    def whole_sum(q):
+        total = acc[q]
+        for d in range(1, outer):
+            along(q, d).wait_recv()
+            total = total + buf_b[q, d - 1]
+        piv[col, piece(q, place)] = total
         for d in range(1, inner):
             around(q, d).start()
         across(q, 0).start()
@@ -177,6 +161,12 @@
             around(q, d).wait_recv()
             across(q, d).start()
 
+    for q in range(panels):
+        layer_sum(q)
+        if q == min(2, panels - 1):
+            whole_sum(0)
+    for q in range(1, min(2, panels)):
+        whole_sum(q)
     forward(0)
     prow[...] = jnp.zeros_like(prow)
     out_ref[...] = jnp.zeros_like(out_ref)
@@ -197,9 +187,6 @@
     eye = jnp.where(same, 1.0, 0.0)
 
     def panel(q, carry):
-        @pl.when(q + 1 < panels)
-        def _():
-            forward(q + 1)
         for d in range(inner):
             across(q, d).wait_recv()
         span = pl.ds(pl.multiple_of(q * size, size), size)
@@ -228,6 +215,14 @@
                   + RIDGE_LEVEL * eye - dot(prow[q], prow[q]))
         e = inv.at[q]
         e[...] = eye
+
+        @pl.when(q + 2 < panels)
+        def _():
+            whole_sum(q + 2)
+
+        @pl.when(q + 1 < panels)
+        def _():
+            forward(q + 1)
         ids = owners[pl.ds(q, 1), :] * here + slots[pl.ds(q, 1), :]
         columns = (entries(points[mine, :], other_points[...], factor[mine, :], other_factor[...], ps, po,
                            own_norm, row_norm)
@@ -235,88 +230,90 @@
         factor_block(size, a, e, rows, None, wide)
         out_ref[:, span] = lax.dot_general(columns, e[...], NT, precision=HIGH,
                                            preferred_element_type=f32).astype(bf16)
+        swap_panel(q).start()
         return carry
 
     lax.fori_loop(0, panels, panel, 0)
     for c in step_a + swap:
         c.wait_send()
     for q in range(panels):
-        @pl.when(layer != q)
-        def _():
-            to_owner(q).wait_send()
-
-        @pl.when(layer == q)
-        def _():
-            for d in range(1, outer):
-                spread(q, (q + d) % outer).wait_send()
+        swap_panel(q).wait()
+        for d in range(1, outer):
+            along(q, d).wait_send()
         for d in range(1, inner):
             around(q, d).wait_send()
         for d in range(inner):
             across(q, d).wait_send()
 
 
-def gram_kernel(inner, outer, scale, built, factor, weights, own_cols, gram,
-                theirs, part, keep, buf_a, mid, acc, buf_b,
-                a_send, a_recv, b_send, b_recv, x_send, x_recv):
+def gram_kernel(inner, outer, scale, built, theirs, factor, weights, own_cols, gram_old, gram_new,
+                turned, part, acc, mid, buf_a, buf_b, a_send, a_recv, b_send, b_recv):
     me = lax.axis_index("rows")
     col = lax.axis_index("cols")
     place, layer = me % inner, me // inner
-    half, wide = built.shape
+    half, count = built.shape
     width = own_cols.shape[1]
     rank = factor.shape[1]
-    chunk = gram.shape[0]
-    f32 = jnp.float32
+    chunk = gram_old.shape[0]
+    pieces = acc.shape[0]
+    wide = acc.shape[3]
+    size = weights.shape[1]
+    f32, bf16 = jnp.float32, jnp.bfloat16
     greet(me, col, inner, outer)
-    swap = remote(built, theirs, x_send, x_recv, me, 1 - col)
-    swap.start()
     lanes = pl.ds(pl.multiple_of(col * width, 128), width)
-
-    def add(source, which, start):
+    for source, which in ((built, col), (theirs, 1 - col)):
         span = pl.ds(pl.multiple_of(which * half, 16), half)
-        weighted = (source[...].astype(f32) * weights[span, :]).astype(jnp.bfloat16)
-        own = source[:, lanes]
-        own_cols[span, :] = own
-        old = lax.dot_general(weighted, factor[span, :], TN, preferred_element_type=f32)
-        new = lax.dot_general(weighted, own, TN, preferred_element_type=f32)
-        if start:
-            keep[:, :rank] = old
-            keep[:, rank:] = new
+        own_cols[span, :] = source[:, lanes]
+        for i in range(half // size):
+            row = weights[pl.ds(which * (half // size) + i, 1), :]
+            level = jnp.transpose(jnp.broadcast_to(row, (size, size)))[:, 0:1]
+            block = source[i * size:(i + 1) * size, :].astype(f32) * level
+            first = pl.multiple_of(which * half + i * size, size)
+            turned[:, pl.ds(first, size)] = jnp.transpose(block).astype(bf16)
+
+    def step_a(j, d):
+        p = (place + d) % inner
+        return remote(part.at[j, :, p], buf_a.at[j, d - 1], a_send.at[j, d - 1], a_recv.at[j, d - 1],
+                      layer * inner + p, col)
+
+    def step_b(j, d):
+        z = (layer + d) % outer
+        return remote(mid.at[j, z], buf_b.at[j, d - 1], b_send.at[j, d - 1], b_recv.at[j, d - 1],
+                      z * inner + place, col)
+
+    kept = []
+    for j in range(pieces):
+        if j * wide < rank:
+            right = factor[:, j * wide:(j + 1) * wide]
         else:
-            keep[:, :rank] = (keep[:, :rank] + old) * scale
-            keep[:, rank:] = (keep[:, rank:] + new) * scale
-
-    add(built, col, True)
-    swap.wait_recv()
-    add(theirs, 1 - col, False)
-    for z in range(outer):
-        for p in range(inner):
-            first = (z * inner + p) * chunk
-            part[z, p] = keep[first:first + chunk, :].astype(jnp.bfloat16)
-    stage = []
-    for d in range(1, inner):
-        p = (place + d) % inner
-        c = remote(part.at[:, p], buf_a.at[d - 1], a_send.at[d - 1], a_recv.at[d - 1], layer * inner + p, col)
-        c.start()
-        stage.append(c)
-    for z in range(outer):
-        acc[z] = keep[pl.ds(pl.multiple_of((z * inner + place) * chunk, 8), chunk), :]
-    for d in range(1, inner):
-        stage[d - 1].wait_recv()
-        acc[...] = acc[...] + buf_a[d - 1].astype(f32)
-    mid[...] = acc[...].astype(jnp.bfloat16)
-    second = []
-    for d in range(1, outer):
-        z = (layer + d) % outer
-        c = remote(mid.at[z], buf_b.at[d - 1], b_send.at[d - 1], b_recv.at[d - 1], z * inner + place, col)
-        c.start()
-        second.append(c)
-    total = acc[layer]
-    for d in range(1, outer):
-        second[d - 1].wait_recv()
-        total = total + buf_b[d - 1].astype(f32)
-    gram[...] = total
-    for c in stage + second + [swap]:
-        c.wait_send()
+            right = own_cols[:, j * wide - rank:(j + 1) * wide - rank]
+        block = jnp.dot(turned[...], right, preferred_element_type=f32) * scale
+        part[j] = block.reshape(outer, inner, chunk, wide).astype(bf16)
+        for d in range(1, inner):
+            step_a(j, d).start()
+    for j in range(pieces):
+        total = part[j, :, place].astype(f32)
+        for d in range(1, inner):
+            step_a(j, d).wait_recv()
+            total = total + buf_a[j, d - 1].astype(f32)
+        acc[j] = total
+        mid[j] = total.astype(bf16)
+        for d in range(1, outer):
+            step_b(j, d).start()
+    for j in range(pieces):
+        total = acc[j, layer]
+        for d in range(1, outer):
+            step_b(j, d).wait_recv()
+            total = total + buf_b[j, d - 1].astype(f32)
+        if j * wide < rank:
+            gram_old[:, j * wide:(j + 1) * wide] = total
+        else:
+            gram_new[:, j * wide - rank:(j + 1) * wide - rank] = total
+    for j in range(pieces):
+        for d in range(1, inner):
+            step_a(j, d).wait_send()
+        for d in range(1, outer):
+            step_b(j, d).wait_send()
 
 
 def body(points, factor, weights, pivot_slots, pivot_owners):
@@ -338,49 +335,48 @@
     split = 4 if rows % 16 == 0 else inner
     layers = rows // split
     piece = size // split
-    built = pl.pallas_call(
+    built, built_other = pl.pallas_call(
         functools.partial(panel_kernel, split, layers),
-        out_shape=jax.ShapeDtypeStruct((half, count), bf16),
-        in_specs=[vm] * 4, out_specs=vm, name="panels",
+        out_shape=(jax.ShapeDtypeStruct((half, count), bf16),) * 2,
+        in_specs=[vm] * 4, out_specs=(vm,) * 2, name="panels",
         scratch_shapes=[
             VMEM((count, width), bf16), VMEM((2, count, width), bf16),
             VMEM((half, fw), bf16), VMEM((half, rank), bf16),
             VMEM((panels, split - 1, piece, width), bf16),
-            VMEM((layers, piece, width), bf16),
+            VMEM((panels, layers - 1, piece, width), bf16),
             VMEM((panels, piece, width), bf16),
             VMEM((panels, size, count), bf16),
             VMEM((panels, size, size), f32), VMEM((panels, size, size), f32), VMEM((size, size), f32),
             VMEM((BLOCK, size), f32), VMEM((BLOCK, BLOCK, size), f32),
-            sem(panels, split - 1), sem(panels, split - 1), sem(panels), sem(layers),
-            sem(layers), sem(panels), sem(panels, split - 1), sem(panels, split - 1),
+            sem(panels, split - 1), sem(panels, split - 1), sem(panels, layers - 1), sem(panels, layers - 1),
+            sem(panels), sem(panels), sem(panels, split - 1), sem(panels, split - 1),
             sem(panels, split), sem(panels, split), sem(2), sem(2),
         ],
         compiler_params=pltpu.CompilerParams(collective_id=0, has_side_effects=True, vmem_limit_bytes=limit),
     )(pivot_slots, pivot_owners, points, factor)
 
     scale = size / math.sqrt(here * rows)
-    gw = rank + count // 2
-    own_cols, gram = pl.pallas_call(
+    wide = math.gcd(rank, count // 2)
+    pieces = (rank + count // 2) // wide
+    return pl.pallas_call(
         functools.partial(gram_kernel, inner, outer, scale),
         out_shape=(
             jax.ShapeDtypeStruct((here, count // 2), bf16),
-            jax.ShapeDtypeStruct((chunk, gw), f32),
+            jax.ShapeDtypeStruct((chunk, rank), f32),
+            jax.ShapeDtypeStruct((chunk, count // 2), f32),
         ),
-        in_specs=[vm] * 3, out_specs=(vm,) * 2, name="gram",
+        in_specs=[vm] * 4, out_specs=(vm,) * 3, name="gram",
         scratch_shapes=[
-            VMEM((half, count), bf16),
-            VMEM((outer, inner, chunk, gw), bf16),
-            VMEM((count, gw), f32),
-            VMEM((inner - 1, outer, chunk, gw), bf16),
-            VMEM((outer, chunk, gw), bf16),
-            VMEM((outer, chunk, gw), f32),
-            VMEM((outer - 1, chunk, gw), bf16),
-            sem(inner - 1), sem(inner - 1), sem(outer - 1), sem(outer - 1),
-            pltpu.SemaphoreType.DMA, pltpu.SemaphoreType.DMA,
+            VMEM((count, here), bf16),
+            VMEM((pieces, outer, inner, chunk, wide), bf16),
+            VMEM((pieces, outer, chunk, wide), f32),
+            VMEM((pieces, outer, chunk, wide), bf16),
+            VMEM((pieces, inner - 1, outer, chunk, wide), bf16),
+            VMEM((pieces, outer - 1, chunk, wide), bf16),
+            sem(pieces, inner - 1), sem(pieces, inner - 1), sem(pieces, outer - 1), sem(pieces, outer - 1),
         ],
         compiler_params=pltpu.CompilerParams(collective_id=1, has_side_effects=True, vmem_limit_bytes=limit),
-    )(built, factor, weights[:, None])
-    return own_cols, gram[:, :rank], gram[:, rank:]
+    )(built, built_other, factor, weights.reshape(here // size, size))
 
 
 def solution(mesh):

time: 93.1 us -> 87.9 us (0.944)
  local copies, waits for them, and re-layouts: 5.89 us -> 3.25 us
  Pallas kernels: 86.2 us -> 83.8 us
    slice x2 -> x0, local copies, waits for them, and re-layouts: 2.85 us -> none  [body(): return (own_cols, gram[:, :rank], gram[:, rank:])]
    pallas_call x1, Pallas kernels: 25.3 us -> 22.8 us  [body(): pl.pallas_call(functools.partial(gram_kernel, inner, outer, scale), out_s...]
    unnamed x3 -> x7, local copies, waits for them, and re-layouts: 1.97 us -> 3.25 us
    broadcast_in_dim x1 -> x0, local copies, waits for them, and re-layouts: 1.07 us -> none  [body(): weights[:, None]]
where the time goes in v3:
time: 87.9 us; the launch traced here: 87.7 us
  Pallas kernels  83.8 us (95%)
  local copies, waits for them, and re-layouts  3.25 us (4%)
    pallas_call x1, Pallas kernels, body(): pl.pallas_call(functools.partial(panel_kernel, split, layers), out_shape=...  61 us
    pallas_call x1, Pallas kernels, body(): pl.pallas_call(functools.partial(gram_kernel, inner, outer, scale), out_s...  22.8 us
    unnamed x7, local copies, waits for them, and re-layouts  3.25 us

profile of v3, /device:TPU:0, one launch (start us, length us, event | category | flops | bytes accessed | tf_op | source)
XLA Modules:
  0.0 87.7 jit_solution(10288637064071650225)
XLA Ops:
  0.6 61.0 %panels.1 = (bf16[640,512]{1,0:T(8,128)(2,1)}, bf16[640,512]{1,0:T(8,128)(2,1)}) custom-call(s32[4,128]{1,0:T(4,128)} %slots.1, s32[4,128]{1,0:T(4,128)} %owners.1, bf16[1280,256]{1,0:T(8,128)(2,1)} %points.1, bf16[1280,512]{1,0:T(8,128)(2,1)} %factor.3), custom_call_target="tpu_custom_call" | custom-call | tf_op jit(solution)/shard_map/panels/pallas_call | solution.py:338
  61.7 22.8 %gram.1 = (bf16[1280,256]{1,0:T(8,128)(2,1)}, f32[32,512]{1,0:T(8,128)}, f32[32,256]{1,0:T(8,128)}) custom-call(bf16[640,512]{1,0:T(8,128)(2,1)} %get-tuple-element.5.built, bf16[640,512]{1,0:T(8,128)(2,1)} %get-tuple-element.6.theirs, bf16[1280,512]{1,0:T(8,128)(2,1)} %factor.3, f32[10,128]{1,0:T(8,128)} %bitcast.1), custom_call_target="tpu_custom_call" | custom-call | tf_op jit(solution)/shard_map/gram/pallas_call | solution.py:361
  84.5 0.0 copy-start
  84.5 0.0 copy-start.1
  84.5 2.0 %copy.11 = bf16[1280,256]{1,0:T(8,128)(2,1)} copy(bf16[1280,256]{1,0:T(8,128)(2,1)} %get-tuple-element.10) | data formatting | bytes 1310720
  86.5 0.0 copy-done
  86.5 0.6 copy.12
  87.1 0.0 copy-done.1
  87.1 0.6 copy.13
Async XLA Ops:
  84.5 2.0 %copy-start = (f32[32,512]{1,0:T(8,128)S(1)}, f32[32,512]{1,0:T(8,128)}, u32[]{:S(2)}) copy-start(f32[32,512]{1,0:T(8,128)} %get-tuple-element.11) | copy-start | bytes 196612
  84.5 2.6 %copy-start.1 = (f32[32,256]{1,0:T(8,128)S(1)}, f32[32,256]{1,0:T(8,128)}, u32[]{:S(2)}) copy-start(f32[32,256]{1,0:T(8,128)} %get-tuple-element.12) | copy-start | bytes 98308

commit v4 on v3

--- a/solution.py
+++ b/solution.py
@@ -14,13 +14,6 @@
 HIGH = lax.Precision.HIGHEST
 NT = (((1,), (1,)), ((), ()))
 TN = (((0,), (0,)), ((), ()))
-
-
-def inner_size(rows):
-    inner = 1
-    while inner * inner * 4 <= rows:
-        inner *= 2
-    return inner
 
 
 def remote(src, dst, send, recv, row, col):
@@ -77,7 +70,9 @@
             e[after:, :] = rest_e
 
 
-def panel_kernel(inner, outer, slots, owners, points, factor, out_ref, other_ref,
+def panel_kernel(inner, outer, scale_by, slots, owners, points, factor, weights, own_cols, gram_old, gram_new,
+                 out_ref, other_ref, level_t, gp, ga, gacc, gmid, gb, nw, na, nacc, nmid, nb,
+                 ga_send, ga_recv, gb_send, gb_recv, na_send, na_recv, nb_send, nb_recv,
                  part, piv, other_points, other_factor, buf_a, buf_b, acc,
                  prow, inv, norms, a, rows, wide,
                  a_send, a_recv, b_send, b_recv, f_send, f_recv,
@@ -165,9 +160,9 @@
         layer_sum(q)
         if q == min(2, panels - 1):
             whole_sum(0)
+    forward(0)
     for q in range(1, min(2, panels)):
         whole_sum(q)
-    forward(0)
     prow[...] = jnp.zeros_like(prow)
     out_ref[...] = jnp.zeros_like(out_ref)
     for c in swap:
@@ -185,6 +180,59 @@
     own_ids = lax.broadcasted_iota(jnp.int32, (half, size), 0) + (me * here + col * half)
     same = lax.broadcasted_iota(jnp.int32, (size, size), 0) == lax.broadcasted_iota(jnp.int32, (size, size), 1)
     eye = jnp.where(same, 1.0, 0.0)
+
+    runs = gp.shape[1]
+    lines = gp.shape[3]
+    width = own_cols.shape[1]
+    wide_lanes = pl.ds(pl.multiple_of(col * width, 128), width)
+
+    def gram_a(k, d):
+        p = (place + d) % inner
+        return remote(gp.at[k, :, p], ga.at[k, d - 1], ga_send.at[k, d - 1], ga_recv.at[k, d - 1],
+                      layer * inner + p, col)
+
+    def gram_b(k, i):
+        target = k * runs + i
+        slot = (layer - target + 2 * outer - 1) % outer
+        return remote(gmid.at[k, i], gb.at[slot], gb_send.at[k, i], gb_recv.at[slot], target * inner + place, col)
+
+    def gram_got(d):
+        return remote(gmid.at[0, 0], gb.at[d - 1], gb_send.at[0, 0], gb_recv.at[d - 1],
+                      ((layer + d) % outer) * inner + place, col)
+
+    def new_a(d):
+        p = (place + d) % inner
+        return remote(nw.at[:, p], na.at[d - 1], na_send.at[d - 1], na_recv.at[d - 1], layer * inner + p, col)
+
+    def new_b(d):
+        z = (layer + d) % outer
+        return remote(nmid.at[z], nb.at[d - 1], nb_send.at[d - 1], nb_recv.at[d - 1], z * inner + place, col)
+
+    def gram_block(k):
+        swap_panel(k).wait_recv()
+        lanes = pl.ds(pl.multiple_of(k * size, size), size)
+        for source, which in ((out_ref, col), (other_ref, 1 - col)):
+            for i in range(half // size):
+                level = turned(weights[pl.ds(which * (half // size) + i, 1), :])[:, 0:1]
+                block = source[i * size:(i + 1) * size, lanes].astype(f32) * level
+                first = pl.multiple_of(which * half + i * size, size)
+                level_t[lanes, pl.ds(first, size)] = jnp.transpose(block).astype(bf16)
+        block = jnp.dot(level_t[lanes, :], factor[...], preferred_element_type=f32) * scale_by
+        gp[k] = block.reshape(runs, inner, lines, factor.shape[1]).astype(bf16)
+        for d in range(1, inner):
+            gram_a(k, d).start()
+
+    def gram_sum(k):
+        total = gp[k, :, place].astype(f32)
+        for d in range(1, inner):
+            gram_a(k, d).wait_recv()
+            total = total + ga[k, d - 1].astype(f32)
+        gacc[k] = total
+        gmid[k] = total.astype(bf16)
+        for i in range(runs):
+            @pl.when(layer != k * runs + i)
+            def _():
+                gram_b(k, i).start()
 
     def panel(q, carry):
         for d in range(inner):
@@ -223,6 +271,14 @@
         @pl.when(q + 1 < panels)
         def _():
             forward(q + 1)
+
+        @pl.when(q > 1)
+        def _():
+            gram_sum(q - 2)
+
+        @pl.when(q > 0)
+        def _():
+            gram_block(q - 1)
         ids = owners[pl.ds(q, 1), :] * here + slots[pl.ds(q, 1), :]
         columns = (entries(points[mine, :], other_points[...], factor[mine, :], other_factor[...], ps, po,
                            own_norm, row_norm)
@@ -234,86 +290,54 @@
         return carry
 
     lax.fori_loop(0, panels, panel, 0)
+    if panels > 1:
+        gram_sum(panels - 2)
+    gram_block(panels - 1)
+    for source, which in ((out_ref, col), (other_ref, 1 - col)):
+        own_cols[pl.ds(pl.multiple_of(which * half, 16), half), :] = source[:, wide_lanes]
+    block = jnp.dot(level_t[...], own_cols[...], preferred_element_type=f32) * scale_by
+    nw[...] = block.reshape(outer, inner, lines, width).astype(bf16)
+    for d in range(1, inner):
+        new_a(d).start()
+    gram_sum(panels - 1)
+    total = nw[:, place].astype(f32)
+    for d in range(1, inner):
+        new_a(d).wait_recv()
+        total = total + na[d - 1].astype(f32)
+    nacc[...] = total
+    nmid[...] = total.astype(bf16)
+    for d in range(1, outer):
+        new_b(d).start()
+    total = gacc[layer // runs, layer % runs]
+    for d in range(1, outer):
+        gram_got(d).wait_recv()
+        total = total + gb[d - 1].astype(f32)
+    gram_old[...] = total
+    total = nacc[layer]
+    for d in range(1, outer):
+        new_b(d).wait_recv()
+        total = total + nb[d - 1].astype(f32)
+    gram_new[...] = total
+    for d in range(1, inner):
+        new_a(d).wait_send()
+    for d in range(1, outer):
+        new_b(d).wait_send()
     for c in step_a + swap:
         c.wait_send()
     for q in range(panels):
-        swap_panel(q).wait()
+        swap_panel(q).wait_send()
+        for d in range(1, inner):
+            gram_a(q, d).wait_send()
+        for i in range(runs):
+            @pl.when(layer != q * runs + i)
+            def _():
+                gram_b(q, i).wait_send()
         for d in range(1, outer):
             along(q, d).wait_send()
         for d in range(1, inner):
             around(q, d).wait_send()
         for d in range(inner):
             across(q, d).wait_send()
-
-
-def gram_kernel(inner, outer, scale, built, theirs, factor, weights, own_cols, gram_old, gram_new,
-                turned, part, acc, mid, buf_a, buf_b, a_send, a_recv, b_send, b_recv):
-    me = lax.axis_index("rows")
-    col = lax.axis_index("cols")
-    place, layer = me % inner, me // inner
-    half, count = built.shape
-    width = own_cols.shape[1]
-    rank = factor.shape[1]
-    chunk = gram_old.shape[0]
-    pieces = acc.shape[0]
-    wide = acc.shape[3]
-    size = weights.shape[1]
-    f32, bf16 = jnp.float32, jnp.bfloat16
-    greet(me, col, inner, outer)
-    lanes = pl.ds(pl.multiple_of(col * width, 128), width)
-    for source, which in ((built, col), (theirs, 1 - col)):
-        span = pl.ds(pl.multiple_of(which * half, 16), half)
-        own_cols[span, :] = source[:, lanes]
-        for i in range(half // size):
-            row = weights[pl.ds(which * (half // size) + i, 1), :]
-            level = jnp.transpose(jnp.broadcast_to(row, (size, size)))[:, 0:1]
-            block = source[i * size:(i + 1) * size, :].astype(f32) * level
-            first = pl.multiple_of(which * half + i * size, size)
-            turned[:, pl.ds(first, size)] = jnp.transpose(block).astype(bf16)
-
-    def step_a(j, d):
-        p = (place + d) % inner
-        return remote(part.at[j, :, p], buf_a.at[j, d - 1], a_send.at[j, d - 1], a_recv.at[j, d - 1],
-                      layer * inner + p, col)
-
-    def step_b(j, d):
-        z = (layer + d) % outer
-        return remote(mid.at[j, z], buf_b.at[j, d - 1], b_send.at[j, d - 1], b_recv.at[j, d - 1],
-                      z * inner + place, col)
-
-    kept = []
-    for j in range(pieces):
-        if j * wide < rank:
-            right = factor[:, j * wide:(j + 1) * wide]
-        else:
-            right = own_cols[:, j * wide - rank:(j + 1) * wide - rank]
-        block = jnp.dot(turned[...], right, preferred_element_type=f32) * scale
-        part[j] = block.reshape(outer, inner, chunk, wide).astype(bf16)
-        for d in range(1, inner):
-            step_a(j, d).start()
-    for j in range(pieces):
-        total = part[j, :, place].astype(f32)
-        for d in range(1, inner):
-            step_a(j, d).wait_recv()
-            total = total + buf_a[j, d - 1].astype(f32)
-        acc[j] = total
-        mid[j] = total.astype(bf16)
-        for d in range(1, outer):
-            step_b(j, d).start()
-    for j in range(pieces):
-        total = acc[j, layer]
-        for d in range(1, outer):
-            step_b(j, d).wait_recv()
-            total = total + buf_b[j, d - 1].astype(f32)
-        if j * wide < rank:
-            gram_old[:, j * wide:(j + 1) * wide] = total
-        else:
-            gram_new[:, j * wide - rank:(j + 1) * wide - rank] = total
-    for j in range(pieces):
-        for d in range(1, inner):
-            step_a(j, d).wait_send()
-        for d in range(1, outer):
-            step_b(j, d).wait_send()
 
 
 def body(points, factor, weights, pivot_slots, pivot_owners):
@@ -321,8 +345,6 @@
     rank = factor.shape[1]
     panels, size = pivot_slots.shape
     rows = lax.axis_size("rows")
-    inner = inner_size(rows)
-    outer = rows // inner
     count = panels * size
     chunk = count // rows
     width = fw + rank
@@ -332,14 +354,32 @@
     sem = lambda *n: pltpu.SemaphoreType.DMA(n)
     limit = 60 * 1024 * 1024
 
-    split = 4 if rows % 16 == 0 else inner
+    split = rows // panels if rows < panels * panels else panels
     layers = rows // split
     piece = size // split
-    built, built_other = pl.pallas_call(
-        functools.partial(panel_kernel, split, layers),
-        out_shape=(jax.ShapeDtypeStruct((half, count), bf16),) * 2,
-        in_specs=[vm] * 4, out_specs=(vm,) * 2, name="panels",
+    runs = layers // panels
+    share = count // 2
+    scale = size / math.sqrt(here * rows)
+    return pl.pallas_call(
+        functools.partial(panel_kernel, split, layers, scale),
+        out_shape=(
+            jax.ShapeDtypeStruct((here, share), bf16),
+            jax.ShapeDtypeStruct((chunk, rank), f32),
+            jax.ShapeDtypeStruct((chunk, share), f32),
+        ),
+        in_specs=[vm] * 5, out_specs=(vm,) * 3, name="panels",
         scratch_shapes=[
+            VMEM((half, count), bf16), VMEM((half, count), bf16), VMEM((count, here), bf16),
+            VMEM((panels, runs, split, chunk, rank), bf16),
+            VMEM((panels, split - 1, runs, chunk, rank), bf16),
+            VMEM((panels, runs, chunk, rank), f32), VMEM((panels, runs, chunk, rank), bf16),
+            VMEM((layers, chunk, rank), bf16),
+            VMEM((layers, split, chunk, share), bf16),
+            VMEM((split - 1, layers, chunk, share), bf16),
+            VMEM((layers, chunk, share), f32), VMEM((layers, chunk, share), bf16),
+            VMEM((layers - 1, chunk, share), bf16),
+            sem(panels, split - 1), sem(panels, split - 1), sem(panels, runs), sem(layers),
+            sem(split - 1), sem(split - 1), sem(layers - 1), sem(layers - 1),
             VMEM((count, width), bf16), VMEM((2, count, width), bf16),
             VMEM((half, fw), bf16), VMEM((half, rank), bf16),
             VMEM((panels, split - 1, piece, width), bf16),
@@ -353,30 +393,7 @@
             sem(panels, split), sem(panels, split), sem(2), sem(2),
         ],
         compiler_params=pltpu.CompilerParams(collective_id=0, has_side_effects=True, vmem_limit_bytes=limit),
-    )(pivot_slots, pivot_owners, points, factor)
-
-    scale = size / math.sqrt(here * rows)
-    wide = math.gcd(rank, count // 2)
-    pieces = (rank + count // 2) // wide
-    return pl.pallas_call(
-        functools.partial(gram_kernel, inner, outer, scale),
-        out_shape=(
-            jax.ShapeDtypeStruct((here, count // 2), bf16),
-            jax.ShapeDtypeStruct((chunk, rank), f32),
-            jax.ShapeDtypeStruct((chunk, count // 2), f32),
-        ),
-        in_specs=[vm] * 4, out_specs=(vm,) * 3, name="gram",
-        scratch_shapes=[
-            VMEM((count, here), bf16),
-            VMEM((pieces, outer, inner, chunk, wide), bf16),
-            VMEM((pieces, outer, chunk, wide), f32),
-            VMEM((pieces, outer, chunk, wide), bf16),
-            VMEM((pieces, inner - 1, outer, chunk, wide), bf16),
-            VMEM((pieces, outer - 1, chunk, wide), bf16),
-            sem(pieces, inner - 1), sem(pieces, inner - 1), sem(pieces, outer - 1), sem(pieces, outer - 1),
-        ],
-        compiler_params=pltpu.CompilerParams(collective_id=1, has_side_effects=True, vmem_limit_bytes=limit),
-    )(built, built_other, factor, weights.reshape(here // size, size))
+    )(pivot_slots, pivot_owners, points, factor, weights.reshape(here // size, size))
 
 
 def solution(mesh):

time: 87.9 us -> 82.3 us (0.936)
  Pallas kernels: 83.8 us -> 78.2 us
    pallas_call x2 -> x1, Pallas kernels: 83.8 us -> 78.2 us  [body(): pl.pallas_call(functools.partial(panel_kernel, split, layers, scale), out...]
where the time goes in v4:
time: 82.3 us; the launch traced here: 82.1 us
  Pallas kernels  78.2 us (95%)
  local copies, waits for them, and re-layouts  3.25 us (4%)
    pallas_call x1, Pallas kernels, body(): pl.pallas_call(functools.partial(panel_kernel, split, layers, scale), out...  78.2 us
    unnamed x7, local copies, waits for them, and re-layouts  3.25 us

profile of v4, /device:TPU:0, one launch (start us, length us, event | category | flops | bytes accessed | tf_op | source)
XLA Modules:
  0.0 82.1 jit_solution(15425535690768323880)
XLA Ops:
  0.6 78.2 %panels.1 = (bf16[1280,256]{1,0:T(8,128)(2,1)}, f32[32,512]{1,0:T(8,128)}, f32[32,256]{1,0:T(8,128)}) custom-call(s32[4,128]{1,0:T(4,128)} %slots.1, s32[4,128]{1,0:T(4,128)} %owners.1, bf16[1280,256]{1,0:T(8,128)(2,1)} %points.1, bf16[1280,512]{1,0:T(8,128)(2,1)} %factor.1, f32[10,128]{1,0:T(8,128)} %bitcast.1), custom_call_target="tpu_custom_call" | custom-call | tf_op jit(solution)/shard_map/panels/pallas_call | solution.py:363
  78.8 0.0 copy-start
  78.9 0.0 copy-start.1
  78.9 2.0 %copy.11 = bf16[1280,256]{1,0:T(8,128)(2,1)} copy(bf16[1280,256]{1,0:T(8,128)(2,1)} %get-tuple-element.6) | data formatting | bytes 1310720
  80.9 0.0 copy-done
  80.9 0.6 copy.12
  81.5 0.0 copy-done.1
  81.5 0.6 copy.13
Async XLA Ops:
  78.8 2.0 %copy-start = (f32[32,512]{1,0:T(8,128)S(1)}, f32[32,512]{1,0:T(8,128)}, u32[]{:S(2)}) copy-start(f32[32,512]{1,0:T(8,128)} %get-tuple-element.7) | copy-start | bytes 196612
  78.9 2.6 %copy-start.1 = (f32[32,256]{1,0:T(8,128)S(1)}, f32[32,256]{1,0:T(8,128)}, u32[]{:S(2)}) copy-start(f32[32,256]{1,0:T(8,128)} %get-tuple-element.8) | copy-start | bytes 98308

commit v5 on v4

--- a/solution.py
+++ b/solution.py
@@ -39,8 +39,8 @@
         span = slice(first, first + BLOCK)
         strip = a[span, :]
         for k in range(BLOCK):
-            wide[k] = jnp.broadcast_to(strip[:, first + k:first + k + 1], (BLOCK, size))
-        d = {(i, k): wide[k, i:i + 1, :] for i in range(BLOCK) for k in range(i + 1)}
+            wide[first // BLOCK % 2 * BLOCK + k] = jnp.broadcast_to(strip[:, first + k:first + k + 1], (BLOCK, size))
+        d = {(i, k): wide[first // BLOCK % 2 * BLOCK + k, i:i + 1, :] for i in range(BLOCK) for k in range(i + 1)}
         r = [a[first + i:first + i + 1, :] for i in range(BLOCK)]
         s = [e[first + i:first + i + 1, :] for i in range(BLOCK)]
         for k in range(BLOCK):
@@ -54,20 +54,23 @@
                 s[i] = s[i] - d[i, k] * s[k]
                 for m in range(k + 1, i + 1):
                     d[i, m] = d[i, m] - d[i, k] * d[m, k]
+        base = BLOCK * (first // BLOCK % 2)
         for k in range(BLOCK):
-            rows[k:k + 1, :] = r[k]
+            rows[base + k:base + k + 1, :] = r[k]
             e[first + k:first + k + 1, :] = s[k]
         after = first + BLOCK
         if after < size:
-            upper = jnp.transpose(rows[...])
-            rest_a = a[after:, :]
-            rest_e = e[after:, :]
-            for k in range(BLOCK):
-                column = upper[after:, k:k + 1]
-                rest_a = rest_a - column * rows[k:k + 1, :]
-                rest_e = rest_e - column * e[first + k:first + k + 1, :]
-            a[after:, :] = rest_a
-            e[after:, :] = rest_e
+            upper = jnp.transpose(rows[base:base + BLOCK, :])
+            for low, high in ((after, after + BLOCK), (after + BLOCK, size)):
+                if low < high:
+                    rest_a = a[low:high, :]
+                    rest_e = e[low:high, :]
+                    for k in range(BLOCK):
+                        column = upper[low:high, k:k + 1]
+                        rest_a = rest_a - column * rows[base + k:base + k + 1, :]
+                        rest_e = rest_e - column * e[first + k:first + k + 1, :]
+                    a[low:high, :] = rest_a
+                    e[low:high, :] = rest_e
 
 
 def panel_kernel(inner, outer, scale_by, slots, owners, points, factor, weights, own_cols, gram_old, gram_new,
@@ -387,7 +390,7 @@
             VMEM((panels, piece, width), bf16),
             VMEM((panels, size, count), bf16),
             VMEM((panels, size, size), f32), VMEM((panels, size, size), f32), VMEM((size, size), f32),
-            VMEM((BLOCK, size), f32), VMEM((BLOCK, BLOCK, size), f32),
+            VMEM((2 * BLOCK, size), f32), VMEM((2 * BLOCK, BLOCK, size), f32),
             sem(panels, split - 1), sem(panels, split - 1), sem(panels, layers - 1), sem(panels, layers - 1),
             sem(panels), sem(panels), sem(panels, split - 1), sem(panels, split - 1),
             sem(panels, split), sem(panels, split), sem(2), sem(2),

time: 82.3 us -> 82.1 us (level)
  no operation moved by 1% of the time
where the time goes in v5:
time: 82.1 us; the launch traced here: 81.9 us
  Pallas kernels  78 us (95%)
  local copies, waits for them, and re-layouts  3.25 us (4%)
    pallas_call x1, Pallas kernels, body(): pl.pallas_call(functools.partial(panel_kernel, split, layers, scale), out...  78 us
    unnamed x7, local copies, waits for them, and re-layouts  3.25 us

profile of v5, /device:TPU:0, one launch (start us, length us, event | category | flops | bytes accessed | tf_op | source)
XLA Modules:
  0.0 81.9 jit_solution(16690275057398191451)
XLA Ops:
  0.6 78.0 %panels.1 = (bf16[1280,256]{1,0:T(8,128)(2,1)}, f32[32,512]{1,0:T(8,128)}, f32[32,256]{1,0:T(8,128)}) custom-call(s32[4,128]{1,0:T(4,128)} %slots.1, s32[4,128]{1,0:T(4,128)} %owners.1, bf16[1280,256]{1,0:T(8,128)(2,1)} %points.1, bf16[1280,512]{1,0:T(8,128)(2,1)} %factor.1, f32[10,128]{1,0:T(8,128)} %bitcast.1), custom_call_target="tpu_custom_call" | custom-call | tf_op jit(solution)/shard_map/panels/pallas_call | solution.py:366
  78.7 0.0 copy-start
  78.7 0.0 copy-start.1
  78.7 2.0 %copy.11 = bf16[1280,256]{1,0:T(8,128)(2,1)} copy(bf16[1280,256]{1,0:T(8,128)(2,1)} %get-tuple-element.6) | data formatting | bytes 1310720
  80.7 0.0 copy-done
  80.7 0.6 copy.12
  81.3 0.0 copy-done.1
  81.3 0.6 copy.13
Async XLA Ops:
  78.7 2.0 %copy-start = (f32[32,512]{1,0:T(8,128)S(1)}, f32[32,512]{1,0:T(8,128)}, u32[]{:S(2)}) copy-start(f32[32,512]{1,0:T(8,128)} %get-tuple-element.7) | copy-start | bytes 196612
  78.7 2.6 %copy-start.1 = (f32[32,256]{1,0:T(8,128)S(1)}, f32[32,256]{1,0:T(8,128)}, u32[]{:S(2)}) copy-start(f32[32,256]{1,0:T(8,128)} %get-tuple-element.8) | copy-start | bytes 98308
